TPU v7x, 32 devices: a whole 2x2x4 slice. The times are simulated.
32 devices in a mesh: dp: 4 (over y, x), seg: 8 (over z, core).
Axes of the slice: x: 2, y: 2, z: 4, core: 2. Of those that a mesh axis runs over, the one named last changes fastest.
Arguments:
- tokens: bfloat16 [128, 128, 768], P(('dp', 'seg')), may hold values from -6 to 6
- doc_counts: int32 [4, 6], replicated, may hold values from 1 to 24, 32 in all within a row
- pad_mask: int32 [4, 32], replicated, may hold values 0 or 1
- attn_in: bfloat16 [768, 2304], replicated, may hold values from -0.21875 to 0.21875
- attn_proj: bfloat16 [768, 768], replicated, may hold values from -0.625 to 0.625
- norm_attn: float32 [768], replicated, may hold values from 0.5 to 1.5
- ffn_up: bfloat16 [768, 3072], replicated, may hold values from -0.21875 to 0.21875
- ffn_down: bfloat16 [3072, 768], replicated, may hold values from -0.109375 to 0.109375
- norm_ffn: float32 [768], replicated, may hold values from 0.5 to 1.5
- segment_embed: float32 [32, 768], replicated, may hold values from -3 to 3
- cross_in: bfloat16 [768, 2304], replicated, may hold values from -0.21875 to 0.21875
- cross_proj: bfloat16 [768, 768], replicated, may hold values from -0.4375 to 0.4375
- cross_norm_attn: float32 [768], replicated, may hold values from 0.5 to 1.5
- cross_up: bfloat16 [768, 3072], replicated, may hold values from -0.21875 to 0.21875
- cross_down: bfloat16 [3072, 768], replicated, may hold values from -0.109375 to 0.109375
- cross_norm_ffn: float32 [768], replicated, may hold values from 0.5 to 1.5
- cotangent: bfloat16 [128, 128, 768], P(('dp', 'seg')), may hold values from -6 to 6
Outputs:
- output: bfloat16 [128, 128, 768], P(('dp', 'seg'))
- token_grad: bfloat16 [128, 128, 768], P(('dp', 'seg'))
- grad_attn_in: float32 [768, 2304], P('seg', 'dp')
- grad_attn_proj: float32 [768, 768], P('seg', 'dp')
- grad_norm_attn: float32 [768], P('seg')
- grad_ffn_up: float32 [768, 3072], P('seg', 'dp')
- grad_ffn_down: float32 [3072, 768], P('seg', 'dp')
- grad_norm_ffn: float32 [768], P('seg')
- grad_segment_embed: float32 [32, 768], P('dp', 'seg')
- grad_cross_in: float32 [768, 2304], P('seg', 'dp')
- grad_cross_proj: float32 [768, 768], P('seg', 'dp')
- grad_cross_norm_attn: float32 [768], P('seg')
- grad_cross_up: float32 [768, 3072], P('seg', 'dp')
- grad_cross_down: float32 [3072, 768], P('seg', 'dp')
- grad_cross_norm_ffn: float32 [768], P('seg')
Inputs may be any that keep to these rules, and one draw needn't show every extreme that they name: `doc_counts`: the 6 document lengths of each slot sum to 32, and each slot has one of exactly 24 segments. `pad_mask`: 1 marks a padding segment.
All inputs are finite; a program needn't handle non-finite values.
Results may differ from a plain program's by a relative error of at most 0.023.
Values may be sent and summed in bfloat16 or wider, within the bound.
A program may use at most 192 MiB of HBM per device.

v0:
```python
from functools import partial

import jax
import jax.numpy as jnp
from jax import lax
from jax.sharding import PartitionSpec as P

H = 12
HD = 64
SLOT_SEGS = 32


EPSILON = 1e-05
MASKED = -1e30


def matmul(former, latter):
    return jnp.dot(former, latter, preferred_element_type=jnp.float32)


def exact_dot(former, latter):
    return jnp.dot(former, latter, precision=lax.Precision.HIGHEST)


def outer_sum(former, latter):
    return lax.dot_general(
        former, latter, (((0,), (0,)), ((), ())), preferred_element_type=jnp.float32
    )


def back_product(gradient, weight):
    return lax.dot_general(
        gradient, weight, (((1,), (1,)), ((), ())), preferred_element_type=jnp.float32
    )


def norm_forward(summed, gain_row):
    middle = summed - jnp.mean(summed, -1, keepdims=True)
    inverse = lax.rsqrt(jnp.mean(middle * middle, -1, keepdims=True) + EPSILON)
    unit_rows = middle * inverse
    return (unit_rows * gain_row, (unit_rows, inverse))


def norm_backward(state, gain_row, upstream):
    unit_rows, inverse = state
    scaled = upstream * gain_row
    centered = (
        scaled
        - jnp.mean(scaled, -1, keepdims=True)
        - unit_rows * jnp.mean(scaled * unit_rows, -1, keepdims=True)
    )
    return (inverse * centered, jnp.sum(upstream * unit_rows, 0))


def to_heads(columns, batch_size):
    return columns.reshape(batch_size, -1, H, HD)


def attend_forward(queries, key_heads, values, allowed):
    scores = jnp.einsum(
        "bqhe,bkhe->bhqk", queries, key_heads, preferred_element_type=jnp.float32
    ) * HD ** (-0.5)
    if allowed is not None:
        scores = jnp.where(allowed, scores, MASKED)
    attn_probs = jax.nn.softmax(scores, axis=-1)
    probs_low = attn_probs.astype(jnp.bfloat16)
    attended = jnp.einsum("bhqk,bkhe->bqhe", probs_low, values, preferred_element_type=jnp.float32)
    return (attn_probs, probs_low, attended.astype(jnp.bfloat16))


def score_grads(attn_probs, grad_att, values):
    grad_probs = jnp.einsum("bqhe,bkhe->bhqk", grad_att, values, preferred_element_type=jnp.float32)
    return (attn_probs * (grad_probs - jnp.sum(attn_probs * grad_probs, -1, keepdims=True))).astype(
        jnp.bfloat16
    )


def tail_forward(residual, attended, weights):
    attn_proj, norm_attn, ffn_up, ffn_down, norm_ffn = weights
    first_norm, first_state = norm_forward(residual + matmul(attended, attn_proj), norm_attn)
    first_low = first_norm.astype(jnp.bfloat16)
    pre_act = matmul(first_low, ffn_up)
    hidden = jax.nn.gelu(pre_act, approximate=False).astype(jnp.bfloat16)
    result, second_state = norm_forward(first_norm + matmul(hidden, ffn_down), norm_ffn)
    return (result, (attended, first_state, first_low, pre_act, hidden, second_state))


def tail_backward(state, weights, upstream):
    attn_proj, norm_attn, ffn_up, ffn_down, norm_ffn = weights
    attended, first_state, first_low, pre_act, hidden, second_state = state
    grad_second, grad_norm_ffn = norm_backward(second_state, norm_ffn, upstream)
    grad_out_low = grad_second.astype(jnp.bfloat16)
    grad_down = outer_sum(hidden, grad_out_low)
    spare, gelu_back = jax.vjp(partial(jax.nn.gelu, approximate=False), pre_act)
    grad_pre = gelu_back(back_product(grad_out_low, ffn_down))[0].astype(jnp.bfloat16)
    grad_up = outer_sum(first_low, grad_pre)
    grad_first = grad_second + back_product(grad_pre, ffn_up)
    grad_residual, grad_norm_attn = norm_backward(first_state, norm_attn, grad_first)
    grad_proj_out = grad_residual.astype(jnp.bfloat16)
    grad_proj = outer_sum(attended, grad_proj_out)
    grad_att = back_product(grad_proj_out, attn_proj).astype(jnp.bfloat16)
    grads = (grad_proj, grad_norm_attn, grad_up, grad_down, grad_norm_ffn)
    factors = (attended, grad_proj_out, first_low, grad_pre, hidden, grad_out_low)
    return (grad_residual, grad_att, grads, factors)


def segment_forward(token_rows, seg_count, weights):
    attn_in = weights[0]
    model_width = token_rows.shape[1]
    packed = matmul(token_rows, attn_in).astype(jnp.bfloat16)
    queries = to_heads(packed[:, :model_width], seg_count)
    key_heads = to_heads(packed[:, model_width : 2 * model_width], seg_count)
    values = to_heads(packed[:, 2 * model_width :], seg_count)
    attn_probs, probs_low, attended = attend_forward(queries, key_heads, values, None)
    result, state = tail_forward(
        token_rows.astype(jnp.float32), attended.reshape(token_rows.shape), weights[1:]
    )
    return (result, (queries, key_heads, values, attn_probs, probs_low, state))


def placement(device, within, span_devs, group_slots, half_count):
    slot_index = (
        device // span_devs + within % half_count + group_slots // 2 * (within // half_count)
    ) % group_slots
    position = within * span_devs + device % span_devs
    return (slot_index, position)


def documents(slot_index, position, counts_group, pads_group):
    chooser = (
        slot_index[:, None] == jnp.arange(counts_group.shape[0], dtype=jnp.int32)[None, :]
    ).astype(jnp.int32)
    doc_sizes = jnp.sum(chooser[:, :, None] * counts_group[None], 1)
    doc_ends = jnp.cumsum(doc_sizes, 1)
    doc_starts = doc_ends - doc_sizes
    document = jnp.sum((doc_ends <= position[:, None]).astype(jnp.int32), 1)
    is_first = jnp.any(doc_starts == position[:, None], 1)
    doc_index = jnp.arange(doc_sizes.shape[1], dtype=jnp.int32)
    doc_begin = jnp.sum(jnp.where(doc_index[None] == document[:, None], doc_starts, 0), 1)
    pad_rows = jnp.sum(chooser[:, :, None] * pads_group[None], 1)
    place_index = jnp.arange(pad_rows.shape[1], dtype=jnp.int32)
    is_pad = jnp.sum(jnp.where(place_index[None] == position[:, None], pad_rows, 0), 1)
    return (document, position - doc_begin, (is_pad == 0) | is_first)


def key_terms_of(score_grad, prob_rows, query_heads, att_grad, rows_count):
    model_width = H * HD
    grad_key = jnp.einsum(
        "bhqk,bqhe->bkhe", score_grad, query_heads, preferred_element_type=jnp.float32
    ) * HD ** (-0.5)
    grad_value = jnp.einsum(
        "bhqk,bqhe->bkhe", prob_rows, att_grad, preferred_element_type=jnp.float32
    )
    return jnp.concatenate(
        [grad_key.reshape(rows_count, model_width), grad_value.reshape(rows_count, model_width)], 1
    )


def cross_section(
    cross_base,
    cot_rows,
    queries_at,
    keys_at,
    counts_group,
    pads_group,
    segment_embed,
    weights,
    share_keys,
    return_keys,
):
    cross_in = weights[0]
    tail_weights = weights[1:]
    row_count, model_width = cross_base.shape
    slot_query, place_query = queries_at
    slot_key, place_key = keys_at
    doc_query, rank_query, spare_valid = documents(
        slot_query, place_query, counts_group, pads_group
    )
    doc_key, spare_rank, key_valid = documents(slot_key, place_key, counts_group, pads_group)
    allowed = (
        (slot_query[:, None] == slot_key[None, :])
        & (doc_query[:, None] == doc_key[None, :])
        & key_valid[None, :]
    )
    allowed = allowed[None, None]
    embed_pick = (
        rank_query[:, None] == jnp.arange(segment_embed.shape[0], dtype=jnp.int32)[None, :]
    ).astype(jnp.float32)
    cross_input = cross_base + exact_dot(embed_pick, segment_embed)
    cross_low = cross_input.astype(jnp.bfloat16)
    cross_packed = matmul(cross_low, cross_in).astype(jnp.bfloat16)
    cross_query = to_heads(cross_packed[:, :model_width], 1)
    gathered = share_keys(cross_packed[:, model_width:])
    cross_keys = to_heads(gathered[:, :model_width], 1)
    cross_values = to_heads(gathered[:, model_width:], 1)
    cross_probs, cross_probs_low, cross_att = attend_forward(
        cross_query, cross_keys, cross_values, allowed
    )
    cross_result, cross_state = tail_forward(
        cross_input, cross_att.reshape(row_count, model_width), tail_weights
    )
    cross_grad_in, cross_grad_att, cross_tail_grads, cross_factors = tail_backward(
        cross_state, tail_weights, cot_rows
    )
    cross_att_grad = to_heads(cross_grad_att, 1)
    cross_scores = score_grads(cross_probs, cross_att_grad, cross_values)
    cross_grad_query = jnp.einsum(
        "bhqk,bkhe->bqhe", cross_scores, cross_keys, preferred_element_type=jnp.float32
    ) * HD ** (-0.5)
    grad_kv = return_keys(cross_scores, cross_probs_low, cross_query, cross_att_grad)
    cross_grad_packed = jnp.concatenate(
        [cross_grad_query.reshape(row_count, model_width), grad_kv], 1
    ).astype(jnp.bfloat16)
    grad_cross_input = cross_grad_in + back_product(cross_grad_packed, cross_in)
    grad_embed = lax.dot_general(
        embed_pick, grad_cross_input, (((0,), (0,)), ((), ())), precision=lax.Precision.HIGHEST
    )
    return (
        cross_result,
        grad_cross_input,
        grad_embed,
        cross_low,
        cross_grad_packed,
        cross_tail_grads,
        cross_factors,
    )


def on_device(
    tokens,
    doc_counts,
    pad_mask,
    attn_in,
    attn_proj,
    norm_attn,
    ffn_up,
    ffn_down,
    norm_ffn,
    segment_embed,
    cross_in,
    cross_proj,
    cross_norm_attn,
    cross_up,
    cross_down,
    cross_norm_ffn,
    cotangent,
):
    seg_count, seg_length, model_width = tokens.shape
    row_count = seg_count * seg_length
    token_rows = tokens.reshape(row_count, model_width)
    seg_weights = (attn_in, attn_proj, norm_attn, ffn_up, ffn_down, norm_ffn)
    cross_weights = (cross_in, cross_proj, cross_norm_attn, cross_up, cross_down, cross_norm_ffn)
    seg_result, seg_state = segment_forward(token_rows, seg_count, seg_weights)
    seg_cube = seg_result.reshape(seg_count, seg_length, model_width)
    members = lax.axis_size("seg")
    member = lax.axis_index("seg")
    group_index = lax.axis_index("dp")
    span_devs = SLOT_SEGS // seg_count
    group_slots = members // span_devs
    half_count = seg_count // 2
    counts_group = lax.dynamic_slice_in_dim(doc_counts, group_index * group_slots, group_slots, 0)
    pads_group = lax.dynamic_slice_in_dim(pad_mask, group_index * group_slots, group_slots, 0)
    own_rows = jnp.arange(seg_count, dtype=jnp.int32)
    cross_base = seg_cube[:, 0, :]
    cot_first = cotangent[:, 0, :]
    queries_at = placement(member, own_rows, span_devs, group_slots, half_count)
    key_rows_all = jnp.arange(members * seg_count, dtype=jnp.int32)
    keys_at = placement(
        key_rows_all // seg_count, key_rows_all % seg_count, span_devs, group_slots, half_count
    )

    def share_keys(key_rows):
        return lax.all_gather(key_rows, "seg", axis=0, tiled=True)

    def return_keys(score_grad, prob_rows, query_heads, att_grad):
        return lax.psum_scatter(
            key_terms_of(
                score_grad, prob_rows, query_heads, att_grad, lax.axis_size("seg") * seg_count
            ),
            "seg",
            scatter_dimension=0,
            tiled=True,
        )

    (
        cross_result,
        grad_cross_input,
        grad_embed,
        cross_low,
        cross_grad_packed,
        cross_tail_grads,
        cross_factors,
    ) = cross_section(
        cross_base,
        cot_first.astype(jnp.float32),
        queries_at,
        keys_at,
        counts_group,
        pads_group,
        segment_embed,
        cross_weights,
        share_keys,
        return_keys,
    )
    cross_result_low = cross_result.astype(jnp.bfloat16)
    output = jnp.concatenate(
        [cross_result_low[:, None, :], seg_cube[:, 1:, :].astype(jnp.bfloat16)], 1
    )
    upstream = cotangent.astype(jnp.float32)
    score_scale = HD ** (-0.5)
    seg_upstream = jnp.concatenate([grad_cross_input[:, None, :], upstream[:, 1:, :]], 1).reshape(
        row_count, model_width
    )
    queries, key_heads, values, attn_probs, probs_low, tail_state = seg_state
    grad_residual, grad_att, seg_tail_grads, spare_factors = tail_backward(
        tail_state, seg_weights[1:], seg_upstream
    )
    grad_att_heads = to_heads(grad_att, seg_count)
    grad_scores = score_grads(attn_probs, grad_att_heads, values)
    grad_query = (
        jnp.einsum("bhqk,bkhe->bqhe", grad_scores, key_heads, preferred_element_type=jnp.float32)
        * score_scale
    )
    grad_key = (
        jnp.einsum("bhqk,bqhe->bkhe", grad_scores, queries, preferred_element_type=jnp.float32)
        * score_scale
    )
    grad_value = jnp.einsum(
        "bhqk,bqhe->bkhe", probs_low, grad_att_heads, preferred_element_type=jnp.float32
    )
    grad_packed = jnp.concatenate(
        [
            grad_query.reshape(row_count, model_width),
            grad_key.reshape(row_count, model_width),
            grad_value.reshape(row_count, model_width),
        ],
        1,
    ).astype(jnp.bfloat16)
    grad_attn_in = outer_sum(token_rows, grad_packed)
    token_grad = (
        (grad_residual + back_product(grad_packed, attn_in))
        .astype(jnp.bfloat16)
        .reshape(seg_count, seg_length, model_width)
    )
    grad_attn_proj, grad_norm_attn, grad_ffn_up, grad_ffn_down, grad_norm_ffn = seg_tail_grads
    grad_cross_in = outer_sum(cross_low, cross_grad_packed)
    grad_cross_proj, grad_cross_norm_attn, grad_cross_up, grad_cross_down, grad_cross_norm_ffn = (
        cross_tail_grads
    )
    (
        sum_attn_in,
        sum_attn_proj,
        sum_norm_attn,
        sum_ffn_up,
        sum_ffn_down,
        sum_norm_ffn,
        sum_embed,
        sum_cross_in,
        sum_cross_proj,
        sum_cross_norm_attn,
        sum_cross_up,
        sum_cross_down,
        sum_cross_norm_ffn,
    ) = (
        lax.psum_scatter(grad_attn_in, "seg", scatter_dimension=0, tiled=True),
        lax.psum_scatter(grad_attn_proj, "seg", scatter_dimension=0, tiled=True),
        lax.psum_scatter(grad_norm_attn, "seg", scatter_dimension=0, tiled=True),
        lax.psum_scatter(grad_ffn_up, "seg", scatter_dimension=0, tiled=True),
        lax.psum_scatter(grad_ffn_down, "seg", scatter_dimension=0, tiled=True),
        lax.psum_scatter(grad_norm_ffn, "seg", scatter_dimension=0, tiled=True),
        lax.psum_scatter(grad_embed, "seg", scatter_dimension=1, tiled=True),
        lax.psum_scatter(grad_cross_in, "seg", scatter_dimension=0, tiled=True),
        lax.psum_scatter(grad_cross_proj, "seg", scatter_dimension=0, tiled=True),
        lax.psum_scatter(grad_cross_norm_attn, "seg", scatter_dimension=0, tiled=True),
        lax.psum_scatter(grad_cross_up, "seg", scatter_dimension=0, tiled=True),
        lax.psum_scatter(grad_cross_down, "seg", scatter_dimension=0, tiled=True),
        lax.psum_scatter(grad_cross_norm_ffn, "seg", scatter_dimension=0, tiled=True),
    )
    (
        total_attn_in,
        total_attn_proj,
        total_ffn_up,
        total_ffn_down,
        total_embed,
        total_cross_in,
        total_cross_proj,
        total_cross_up,
        total_cross_down,
    ) = (
        lax.psum_scatter(
            sum_attn_in.astype(jnp.bfloat16), "dp", scatter_dimension=1, tiled=True
        ).astype(jnp.float32),
        lax.psum_scatter(
            sum_attn_proj.astype(jnp.bfloat16), "dp", scatter_dimension=1, tiled=True
        ).astype(jnp.float32),
        lax.psum_scatter(
            sum_ffn_up.astype(jnp.bfloat16), "dp", scatter_dimension=1, tiled=True
        ).astype(jnp.float32),
        lax.psum_scatter(
            sum_ffn_down.astype(jnp.bfloat16), "dp", scatter_dimension=1, tiled=True
        ).astype(jnp.float32),
        lax.psum_scatter(
            sum_embed.astype(jnp.bfloat16), "dp", scatter_dimension=0, tiled=True
        ).astype(jnp.float32),
        lax.psum_scatter(
            sum_cross_in.astype(jnp.bfloat16), "dp", scatter_dimension=1, tiled=True
        ).astype(jnp.float32),
        lax.psum_scatter(
            sum_cross_proj.astype(jnp.bfloat16), "dp", scatter_dimension=1, tiled=True
        ).astype(jnp.float32),
        lax.psum_scatter(
            sum_cross_up.astype(jnp.bfloat16), "dp", scatter_dimension=1, tiled=True
        ).astype(jnp.float32),
        lax.psum_scatter(
            sum_cross_down.astype(jnp.bfloat16), "dp", scatter_dimension=1, tiled=True
        ).astype(jnp.float32),
    )
    total_norm_attn, total_norm_ffn, total_cross_norm_attn, total_cross_norm_ffn = lax.psum(
        (sum_norm_attn, sum_norm_ffn, sum_cross_norm_attn, sum_cross_norm_ffn), "dp"
    )
    return (
        output,
        token_grad,
        total_attn_in,
        total_attn_proj,
        total_norm_attn,
        total_ffn_up,
        total_ffn_down,
        total_norm_ffn,
        total_embed,
        total_cross_in,
        total_cross_proj,
        total_cross_norm_attn,
        total_cross_up,
        total_cross_down,
        total_cross_norm_ffn,
    )


def solution(mesh):
    placed = (
        P(("dp", "seg"), None, None),
        P(),
        P(),
        P(),
        P(),
        P(),
        P(),
        P(),
        P(),
        P(),
        P(),
        P(),
        P(),
        P(),
        P(),
        P(),
        P(("dp", "seg"), None, None),
    )
    return jax.shard_map(
        on_device,
        mesh=mesh,
        in_specs=placed,
        out_specs=(
            P(("dp", "seg"), None, None),
            P(("dp", "seg"), None, None),
            P("seg", "dp"),
            P("seg", "dp"),
            P("seg"),
            P("seg", "dp"),
            P("seg", "dp"),
            P("seg"),
            P("dp", "seg"),
            P("seg", "dp"),
            P("seg", "dp"),
            P("seg"),
            P("seg", "dp"),
            P("seg", "dp"),
            P("seg"),
        ),
        check_vma=False,
    )
```

profile of v0, /device:TPU:0, one launch (start us, length us, event | category | flops | bytes accessed | tf_op | source)
XLA Modules:
  0.0 1091.6 jit_solution(13184385459989810623)
XLA Ops:
  10.8 2.5 slice_convert_fusion.1
  15.0 3.1 convolution_convert_fusion
  19.6 2.3 copy.134
  21.9 2.9 reshape.430
  24.8 2.3 copy.135
  27.1 2.5 reshape.431
  29.6 2.3 copy.133
  31.9 2.4 reshape.429
  34.3 2.0 fusion.38
  36.3 3.0 fusion.105
  43.4 20.5 %multiply_convert_fusion = (bf16[512,3072]{1,0:T(8,128)(2,1)S(1)}, f32[512,3072]{1,0:T(8,128)}, f32[512,3072]{1,0:T(8,128)}) fusion(bf16[768,3072]{1,0:T(8,128)(2,1)S(1)} %bitcast.173, f32[512,768]{1,0:T(8,128)S(1)} %get-tuple-element.108, f32[768]{0:T(1024)S(1)} %copy-done.29, f32[512]{0:T(512)S(1)} %add_rsqrt_fusion.1, f32[512]{0:T(512)S(1)} %broadcast_multiply_fusion.4), kind=kOutput, calls=%fused_computation.5 | convolution fusion | flops 2519728128 | bytes 22027264 | tf_op jit(solution)/shard_map/dot_general | solution.py:18
  63.9 2.8 fusion.107
  68.0 1.9 copy-done.3
  73.9 16.8 %all-gather = bf16[8,4,1536]{2,1,0:T(4,128)(2,1)} all-gather(bf16[1,4,1536]{2,1,0:T(4,128)(2,1)S(1)} %slice_bitcast_fusion), channel_id=1, replica_groups=mesh['dp'=4,'seg'=8] {'seg'}, dimensions={0}, use_global_device_ids=true | all-gather | bytes 110592 | tf_op jit(solution)/shard_map/all_gather | solution.py:273
  105.2 3.2 fusion.97
  108.4 3.4 fusion.110
  113.3 3.7 add_convert_fusion.2
  117.1 1.9 multiply_reduce_fusion.10
  123.2 1.8 convolution_bitcast_fusion.2
  139.0 32.2 %all-reduce.9 = bf16[32,1536]{1,0:T(8,128)(2,1)} all-reduce(f32[32,1536]{1,0:T(8,128)} %pad_maximum_fusion.2), channel_id=2, replica_groups=mesh['dp'=4,'seg'=8] {'seg'}, use_global_device_ids=true, to_apply=%region_24.25.clone | all-reduce | flops 49152 | bytes 294912
  174.0 3.2 convolution_add_fusion.5
  180.2 7.2 add_convert_fusion
  187.5 7.1 multiply_reduce_fusion.2
  196.3 2.2 fusion.25
  198.5 2.7 fusion.76
  201.3 4.7 fusion.74
  206.3 3.4 convolution_convert_fusion.2
  209.8 2.3 copy.157
  212.0 2.4 reshape.443
  214.5 3.4 fusion.14
  225.4 4.9 convolution_bitcast_fusion
  230.3 8.0 copy.176
  238.8 8.7 fusion.44
  247.5 6.0 fusion.79
  253.6 8.9 fusion.100
  262.6 5.9 fusion.96
  277.5 73.1 %reduce-scatter.42.cloned.1.call-done = f32[96,2304]{1,0:T(8,128)} async-done(((f32[768,2304]{1,0:T(8,128)}), f32[96,2304]{1,0:T(8,128)}) %reduce-scatter.42.cloned.1.call-update) | async-done | bytes 884752 | tf_op jit(solution)/shard_map/reduce_scatter | solution.py:372
  350.6 2.0 convert_element_type.211
  352.6 2.1 copy.184
  354.7 73.7 %reduce-scatter.52.cloned.1.call-done = f32[96,2304]{1,0:T(8,128)} async-done(((f32[768,2304]{1,0:T(8,128)}), f32[96,2304]{1,0:T(8,128)}) %reduce-scatter.52.cloned.1.call-update) | async-done | bytes 884752
  428.4 2.2 copy.177
  430.7 97.7 %reduce-scatter.40.cloned.1.call-done = f32[384,768]{1,0:T(8,128)} async-done(((f32[3072,768]{1,0:T(8,128)}), f32[384,768]{1,0:T(8,128)}) %reduce-scatter.40.cloned.1.call-update) | async-done | bytes 1179664 | tf_op jit(solution)/shard_map/reduce_scatter | solution.py:369
  528.5 2.1 convert_element_type.207
  530.6 2.1 copy.180
  532.8 95.8 %reduce-scatter.50.cloned.1.call-done = f32[384,768]{1,0:T(8,128)} async-done(((f32[3072,768]{1,0:T(8,128)}), f32[384,768]{1,0:T(8,128)}) %reduce-scatter.50.cloned.1.call-update) | async-done | bytes 1179664 | tf_op jit(solution)/shard_map/reduce_scatter | solution.py:376
  628.6 2.1 convert_element_type.217
  630.7 2.1 copy.188
  633.0 95.8 %reduce-scatter.36.cloned.1.call-done = f32[96,3072]{1,0:T(8,128)} async-done(((f32[768,3072]{1,0:T(8,128)}), f32[96,3072]{1,0:T(8,128)}) %reduce-scatter.36.cloned.1.call-update) | async-done | bytes 1179664 | tf_op jit(solution)/shard_map/reduce_scatter | solution.py:368
  728.8 2.2 convert_element_type.205
  731.0 98.0 %reduce-scatter.46.cloned.1.call-done = f32[96,3072]{1,0:T(8,128)} async-done(((f32[768,3072]{1,0:T(8,128)}), f32[96,3072]{1,0:T(8,128)}) %reduce-scatter.46.cloned.1.call-update) | async-done | bytes 1179664 | tf_op jit(solution)/shard_map/reduce_scatter | solution.py:375
  829.0 2.2 convert_element_type.215
  831.2 2.4 slice.62
  835.6 27.1 %all-reduce.6 = (f32[768]{0:T(1024)}, f32[768]{0:T(1024)}, f32[768]{0:T(1024)}, f32[768]{0:T(1024)}) all-reduce(f32[768]{0:T(1024)} %get-tuple-element.77, f32[768]{0:T(1024)S(1)} %copy-done.54, f32[768]{0:T(1024)} %get-tuple-element.80, f32[768]{0:T(1024)} %get-tuple-element.82), channel_id=7, replica_groups=mesh['dp'=4,'seg'=8] {'seg'}, use_global_device_ids=true, to_apply=%region_35.36.clone | all-reduce | flops 3072 | bytes 24576
  867.9 10.8 all-reduce.7
  878.7 2.2 pad_maximum_fusion.1
  880.9 5.1 add_convert_fusion.1
  886.9 8.1 all-reduce.3
  898.5 15.6 %reduce-scatter.62.cloned.1.call-done = bf16[192,96]{1,0:T(8,128)(2,1)} async-done(((bf16[768,96]{1,0:T(8,128)(2,1)}), bf16[192,96]{1,0:T(8,128)(2,1)}) %reduce-scatter.62.cloned.1.call-update) | async-done | bytes 36880
  917.1 25.2 %reduce-scatter.60.cloned.1.call-done = bf16[576,96]{1,0:T(8,128)(2,1)} async-done(((bf16[2304,96]{1,0:T(8,128)(2,1)}), bf16[576,96]{1,0:T(8,128)(2,1)}) %reduce-scatter.60.cloned.1.call-update) | async-done | bytes 110608
  945.6 25.0 %reduce-scatter.32.cloned.1.call-done = bf16[96,576]{0,1:T(8,128)(2,1)} async-done(((bf16[96,2304]{0,1:T(8,128)(2,1)}), bf16[96,576]{0,1:T(8,128)(2,1)}) %reduce-scatter.32.cloned.1.call-update) | async-done | bytes 110608 | tf_op jit(solution)/shard_map/reduce_scatter | solution.py:390
  972.3 26.4 %reduce-scatter.56.cloned.1.call-done = bf16[192,384]{1,0:T(8,128)(2,1)} async-done(((bf16[768,384]{1,0:T(8,128)(2,1)}), bf16[192,384]{1,0:T(8,128)(2,1)}) %reduce-scatter.56.cloned.1.call-update) | async-done | bytes 147472
  1002.2 24.7 %reduce-scatter.64.cloned.1.call-done = bf16[192,384]{1,0:T(8,128)(2,1)} async-done(((bf16[768,384]{1,0:T(8,128)(2,1)}), bf16[192,384]{1,0:T(8,128)(2,1)}) %reduce-scatter.64.cloned.1.call-update) | async-done | bytes 147472
  1030.4 24.7 %reduce-scatter.38.cloned.1.call-done = bf16[96,768]{1,0:T(8,128)(2,1)} async-done(((bf16[96,3072]{1,0:T(8,128)(2,1)}), bf16[96,768]{1,0:T(8,128)(2,1)}) %reduce-scatter.38.cloned.1.call-update) | async-done | bytes 147472 | tf_op jit(solution)/shard_map/reduce_scatter | solution.py:396
  1056.7 26.5 %reduce-scatter.48.cloned.1.call-done = bf16[96,768]{1,0:T(8,128)(2,1)} async-done(((bf16[96,3072]{1,0:T(8,128)(2,1)}), bf16[96,768]{1,0:T(8,128)(2,1)}) %reduce-scatter.48.cloned.1.call-update) | async-done | bytes 147472 | tf_op jit(solution)/shard_map/reduce_scatter | solution.py:411
  (308 shorter events, 102.5 us)
Async XLA Ops:
  7.2 7.8 copy-start
  7.2 263.4 %reduce-scatter.34.cloned.1.call-start = ((), (), s32[]{:S(2)}) async-start(), calls=%async_computation.18 | async-start | bytes 2654208 | tf_op jit(solution)/shard_map/reduce_scatter | solution.py:366
  7.3 10.8 copy-start.65
  14.7 3.4 copy-start.60
  14.9 52.8 %copy-start.61 = (s32[4]{0:T(128)}, s32[4]{0:T(128)S(1)}, u32[]{:S(2)}) copy-start(s32[4]{0:T(128)S(1)} %fusion.95) | copy-start | bytes 52
  36.3 7.0 slice-start.6
  39.4 3.9 slice-start.7
  42.0 21.8 %slice-start.2 = ((s8[4718592]{0:T(1024)(128)(4,1)}), s8[4194304]{0:T(1024)(128)(4,1)S(1)}, s32[]{:S(2)}) async-start(s8[4718592]{0:T(1024)(128)(4,1)} %bitcast.168), calls=%async_computation.36 | async-start | bytes 8388608
  43.0 20.9 %copy-start.4 = (f32[512,768]{1,0:T(8,128)}, f32[512,768]{1,0:T(8,128)S(1)}, u32[]{:S(2)}) copy-start(f32[512,768]{1,0:T(8,128)S(1)} %get-tuple-element.108) | copy-start | bytes 4718596
  43.0 20.9 %copy-start.39 = (f32[512]{0:T(512)}, f32[512]{0:T(512)S(1)}, u32[]{:S(2)}) copy-start(f32[512]{0:T(512)S(1)} %broadcast_multiply_fusion.4) | copy-start | bytes 6148
  43.3 20.5 %copy-start.44 = (f32[512]{0:T(512)}, f32[512]{0:T(512)S(1)}, u32[]{:S(2)}) copy-start(f32[512]{0:T(512)S(1)} %add_rsqrt_fusion.1) | copy-start | bytes 6148
  43.3 20.5 %slice-start.3 = ((s8[4718592]{0:T(1024)(128)(4,1)}), s8[524288]{0:T(1024)(128)(4,1)S(1)}, s32[]{:S(2)}) async-start(s8[4718592]{0:T(1024)(128)(4,1)} %bitcast.168), calls=%async_computation.37 | async-start | bytes 1048576
  66.7 3.8 copy-start.1
  66.7 3.2 copy-start.3
  67.1 4.7 copy-start.66
  67.4 3.7 copy-start.14
  69.9 35.2 %copy-start.26 = (f32[768]{0:T(1024)S(1)}, f32[768]{0:T(1024)}, u32[]{:S(2)}) copy-start(f32[768]{0:T(1024)} %param.29) | copy-start | bytes 9220
  104.9 14.2 %copy-start.52 = (f32[4]{0:T(128)}, f32[4]{0:T(128)S(1)}, u32[]{:S(2)}) copy-start(f32[4]{0:T(128)S(1)} %broadcast_multiply_fusion.10) | copy-start | bytes 52
  105.1 14.0 %copy-start.53 = (f32[4]{0:T(128)}, f32[4]{0:T(128)S(1)}, u32[]{:S(2)}) copy-start(f32[4]{0:T(128)S(1)} %add_rsqrt_fusion.3) | copy-start | bytes 52
  105.2 11.9 %slice-start = ((s8[4718592]{0:T(1024)(128)(4,1)}), s8[4194304]{0:T(1024)(128)(4,1)S(1)}, s32[]{:S(2)}) async-start(s8[4718592]{0:T(1024)(128)(4,1)} %bitcast.144), calls=%async_computation.34 | async-start | bytes 8388608
  108.4 4.9 copy-start.25
  108.4 3.6 copy-start.48
  108.4 3.6 copy-start.49
  108.4 8.6 slice-start.1
  111.8 7.2 copy-start.27
  111.8 7.2 copy-start.55
  112.0 7.0 copy-start.57
  113.3 5.7 copy-start.43
  113.3 5.7 copy-start.58
  113.3 5.7 copy-start.59
  173.1 4.7 copy-start.11
  173.1 4.7 copy-start.42
  174.0 3.2 copy-start.33
  174.0 4.2 copy-start.2
  174.0 4.2 copy-start.47
  174.0 4.2 copy-start.51
  179.8 7.7 copy-start.10
  180.2 7.3 copy-start.5
  180.2 7.3 copy-start.30
  180.2 7.3 copy-start.40
  180.2 7.3 copy-start.45
  187.5 7.1 copy-start.18
  198.5 75.6 %reduce-scatter.44.cloned.1.call-start = ((), (), s32[]{:S(2)}) async-start(), calls=%async_computation.23 | async-start | bytes 2654208 | tf_op jit(solution)/shard_map/reduce_scatter | solution.py:373
  201.2 149.3 %reduce-scatter.42.cloned.1.call-start = ((), (), s32[]{:S(2)}) async-start(), calls=%async_computation.22 | async-start | bytes 7962624 | tf_op jit(solution)/shard_map/reduce_scatter | solution.py:372
  206.0 222.4 %reduce-scatter.52.cloned.1.call-start = ((), (), s32[]{:S(2)}) async-start(), calls=%async_computation.27 | async-start | bytes 7962624
  214.5 4.1 copy-start.7
  214.5 4.1 copy-start.21
  214.5 4.1 copy-start.22
  214.5 4.1 copy-start.32
  238.3 290.1 %reduce-scatter.40.cloned.1.call-start = ((), (), s32[]{:S(2)}) async-start(), calls=%async_computation.21 | async-start | bytes 10616832 | tf_op jit(solution)/shard_map/reduce_scatter | solution.py:369
  247.5 381.1 %reduce-scatter.50.cloned.1.call-start = ((), (), s32[]{:S(2)}) async-start(), calls=%async_computation.26 | async-start | bytes 10616832 | tf_op jit(solution)/shard_map/reduce_scatter | solution.py:376
  253.5 475.3 %reduce-scatter.36.cloned.1.call-start = ((), (), s32[]{:S(2)}) async-start(), calls=%async_computation.19 | async-start | bytes 10616832 | tf_op jit(solution)/shard_map/reduce_scatter | solution.py:368
  262.5 566.5 %reduce-scatter.46.cloned.1.call-start = ((), (), s32[]{:S(2)}) async-start(), calls=%async_computation.24 | async-start | bytes 10616832 | tf_op jit(solution)/shard_map/reduce_scatter | solution.py:375
  268.5 617.5 %reduce-scatter.58.cloned.1.call-start = ((), (), s32[]{:S(2)}) async-start(), calls=%async_computation.30 | async-start | bytes 442368
  270.5 625.1 %reduce-scatter.54.cloned.1.call-start = ((), (), s32[]{:S(2)}) async-start(), calls=%async_computation.28 | async-start | bytes 245760
  274.0 640.1 %reduce-scatter.62.cloned.1.call-start = ((), (), s32[]{:S(2)}) async-start(), calls=%async_computation.32 | async-start | bytes 245760
  277.4 664.8 %reduce-scatter.60.cloned.1.call-start = ((), (), s32[]{:S(2)}) async-start(), calls=%async_computation.31 | async-start | bytes 737280
  354.7 615.9 %reduce-scatter.32.cloned.1.call-start = ((), (), s32[]{:S(2)}) async-start(), calls=%async_computation.17 | async-start | bytes 737280 | tf_op jit(solution)/shard_map/reduce_scatter | solution.py:390
  430.7 568.1 %reduce-scatter.56.cloned.1.call-start = ((), (), s32[]{:S(2)}) async-start(), calls=%async_computation.29 | async-start | bytes 737280
  532.8 494.1 %reduce-scatter.64.cloned.1.call-start = ((), (), s32[]{:S(2)}) async-start(), calls=%async_computation.33 | async-start | bytes 737280
  632.9 200.8 %copy-start.68 = (u32[32]{0:T(128)S(1)}, u32[32]{0:T(128)}, u32[]{:S(2)}) copy-start(u32[32]{0:T(128)} %constant.295) | copy-start | bytes 388
  632.9 202.7 %copy-start.54 = (f32[768]{0:T(1024)S(1)}, f32[768]{0:T(1024)}, u32[]{:S(2)}) copy-start(f32[768]{0:T(1024)} %get-tuple-element.75) | copy-start | bytes 9220
  632.9 422.2 %reduce-scatter.38.cloned.1.call-start = ((), (), s32[]{:S(2)}) async-start(), calls=%async_computation.20 | async-start | bytes 737280 | tf_op jit(solution)/shard_map/reduce_scatter | solution.py:396
  731.0 352.3 %reduce-scatter.48.cloned.1.call-start = ((), (), s32[]{:S(2)}) async-start(), calls=%async_computation.25 | async-start | bytes 737280 | tf_op jit(solution)/shard_map/reduce_scatter | solution.py:411
  (30 other events, 46.9 us)
Sparse Core Ops, SparseCore 0:
  198.6 35.2 reduce-scatter.33
  236.2 35.9 reduce-scatter.43
  274.5 76.0 reduce-scatter.41
  352.8 75.6 reduce-scatter.51
  430.6 97.8 reduce-scatter.39
  530.6 97.9 reduce-scatter.49
  630.9 97.8 reduce-scatter.35
  731.1 97.8 reduce-scatter.45
  831.3 29.5 reduce-scatter.57
  864.1 22.3 reduce-scatter.53
  889.8 24.2 reduce-scatter.61
  916.8 25.3 reduce-scatter.59
  945.1 25.3 reduce-scatter.31
  973.3 25.3 reduce-scatter.55
  1001.5 25.3 reduce-scatter.63
  1029.6 25.3 reduce-scatter.37
  1057.8 25.3 reduce-scatter.47
where the time goes:
time: 1100 us; the launch traced here: 1090 us
  waiting for transfers between devices  703 us (64%)
  matrix products  131 us (12%)
  local copies, waits for them, and re-layouts  101 us (9%)
  blocking collectives  95 us (9%)
  other arithmetic  43.3 us (4%)
  between operations  17.3 us (2%)
    unnamed x24, waiting for transfers between devices  166 us
    reduce_scatter x1, waiting for transfers between devices, on_device(): lax.psum_scatter(grad_cross_up, 'seg', scatter_dimension=0, tiled=True)  98 us
    reduce_scatter x1, waiting for transfers between devices, on_device(): lax.psum_scatter(grad_ffn_down, 'seg', scatter_dimension=0, tiled=True)  97.7 us
    reduce_scatter x1, waiting for transfers between devices, on_device(): lax.psum_scatter(grad_ffn_up, 'seg', scatter_dimension=0, tiled=True)  95.8 us
    reduce_scatter x1, waiting for transfers between devices, on_device(): lax.psum_scatter(grad_cross_down, 'seg', scatter_dimension=0, tiled=True)  95.8 us
    reduce_scatter x1, waiting for transfers between devices, on_device(): lax.psum_scatter(grad_cross_in, 'seg', scatter_dimension=0, tiled=True)  73.1 us
    unnamed x3, blocking collectives  67.4 us
    unnamed x180, local copies, waits for them, and re-layouts  51.4 us
  transfers between devices with their start and end apart: 17, of which 13 were waited for; matrix products, arithmetic and copies ran while one was open for 12% of the time, Pallas kernels for 0%

commit v1 on v0

v1 whole, which is shorter than its diff:
```python
from functools import partial

import jax
import jax.numpy as jnp
import numpy as np
from jax import lax
from jax.sharding import PartitionSpec as P

H = 12
HD = 64
SLOT_SEGS = 32


EPSILON = 1e-05
MASKED = -1e30


def matmul(former, latter):
    return jnp.dot(former, latter, preferred_element_type=jnp.float32)


def exact_dot(former, latter):
    return jnp.dot(former, latter, precision=lax.Precision.HIGHEST)


def outer_sum(former, latter):
    return lax.dot_general(
        former, latter, (((0,), (0,)), ((), ())), preferred_element_type=jnp.float32
    )


def back_product(gradient, weight):
    return lax.dot_general(
        gradient, weight, (((1,), (1,)), ((), ())), preferred_element_type=jnp.float32
    )


def norm_forward(summed, gain_row):
    middle = summed - jnp.mean(summed, -1, keepdims=True)
    inverse = lax.rsqrt(jnp.mean(middle * middle, -1, keepdims=True) + EPSILON)
    unit_rows = middle * inverse
    return (unit_rows * gain_row, (unit_rows, inverse))


def norm_backward(state, gain_row, upstream):
    unit_rows, inverse = state
    scaled = upstream * gain_row
    centered = (
        scaled
        - jnp.mean(scaled, -1, keepdims=True)
        - unit_rows * jnp.mean(scaled * unit_rows, -1, keepdims=True)
    )
    return (inverse * centered, jnp.sum(upstream * unit_rows, 0))


def to_heads(columns, batch_size):
    return columns.reshape(batch_size, -1, H, HD)


def attend_forward(queries, key_heads, values, allowed):
    scores = jnp.einsum(
        "bqhe,bkhe->bhqk", queries, key_heads, preferred_element_type=jnp.float32
    ) * HD ** (-0.5)
    if allowed is not None:
        scores = jnp.where(allowed, scores, MASKED)
    attn_probs = jax.nn.softmax(scores, axis=-1)
    probs_low = attn_probs.astype(jnp.bfloat16)
    attended = jnp.einsum("bhqk,bkhe->bqhe", probs_low, values, preferred_element_type=jnp.float32)
    return (attn_probs, probs_low, attended.astype(jnp.bfloat16))


def score_grads(attn_probs, grad_att, values):
    grad_probs = jnp.einsum("bqhe,bkhe->bhqk", grad_att, values, preferred_element_type=jnp.float32)
    return (attn_probs * (grad_probs - jnp.sum(attn_probs * grad_probs, -1, keepdims=True))).astype(
        jnp.bfloat16
    )


def tail_forward(residual, attended, weights):
    attn_proj, norm_attn, ffn_up, ffn_down, norm_ffn = weights
    first_norm, first_state = norm_forward(residual + matmul(attended, attn_proj), norm_attn)
    first_low = first_norm.astype(jnp.bfloat16)
    pre_act = matmul(first_low, ffn_up)
    hidden = jax.nn.gelu(pre_act, approximate=False).astype(jnp.bfloat16)
    result, second_state = norm_forward(first_norm + matmul(hidden, ffn_down), norm_ffn)
    return (result, (attended, first_state, first_low, pre_act, hidden, second_state))


def tail_backward(state, weights, upstream):
    attn_proj, norm_attn, ffn_up, ffn_down, norm_ffn = weights
    attended, first_state, first_low, pre_act, hidden, second_state = state
    grad_second, grad_norm_ffn = norm_backward(second_state, norm_ffn, upstream)
    grad_out_low = grad_second.astype(jnp.bfloat16)
    grad_down = outer_sum(hidden, grad_out_low)
    spare, gelu_back = jax.vjp(partial(jax.nn.gelu, approximate=False), pre_act)
    grad_pre = gelu_back(back_product(grad_out_low, ffn_down))[0].astype(jnp.bfloat16)
    grad_up = outer_sum(first_low, grad_pre)
    grad_first = grad_second + back_product(grad_pre, ffn_up)
    grad_residual, grad_norm_attn = norm_backward(first_state, norm_attn, grad_first)
    grad_proj_out = grad_residual.astype(jnp.bfloat16)
    grad_proj = outer_sum(attended, grad_proj_out)
    grad_att = back_product(grad_proj_out, attn_proj).astype(jnp.bfloat16)
    grads = (grad_proj, grad_norm_attn, grad_up, grad_down, grad_norm_ffn)
    factors = (attended, grad_proj_out, first_low, grad_pre, hidden, grad_out_low)
    return (grad_residual, grad_att, grads, factors)


def segment_forward(token_rows, seg_count, weights):
    attn_in = weights[0]
    model_width = token_rows.shape[1]
    packed = matmul(token_rows, attn_in).astype(jnp.bfloat16)
    queries = to_heads(packed[:, :model_width], seg_count)
    key_heads = to_heads(packed[:, model_width : 2 * model_width], seg_count)
    values = to_heads(packed[:, 2 * model_width :], seg_count)
    attn_probs, probs_low, attended = attend_forward(queries, key_heads, values, None)
    result, state = tail_forward(
        token_rows.astype(jnp.float32), attended.reshape(token_rows.shape), weights[1:]
    )
    return (result, (queries, key_heads, values, attn_probs, probs_low, state))


def row_places(groups, members, seg_count):
    span_devs = SLOT_SEGS // seg_count
    group_slots = members // span_devs
    half_count = seg_count // 2
    row = np.arange(groups * members * seg_count)
    device, within = row // seg_count, row % seg_count
    group, member = device // members, device % members
    slot = group * group_slots + (
        member // span_devs + within % half_count + group_slots // 2 * (within // half_count)
    ) % group_slots
    return slot, within * span_devs + member % span_devs


def documents(doc_counts, pad_mask):
    doc_ends = jnp.cumsum(doc_counts, 1)
    doc_starts = doc_ends - doc_counts
    places = jnp.arange(pad_mask.shape[1], dtype=jnp.int32)
    document = jnp.sum((doc_ends[:, None, :] <= places[None, :, None]).astype(jnp.int32), 2)
    is_first = jnp.any(doc_starts[:, None, :] == places[None, :, None], 2)
    doc_index = jnp.arange(doc_counts.shape[1], dtype=jnp.int32)
    doc_begin = jnp.sum(
        jnp.where(doc_index[None, None] == document[:, :, None], doc_starts[:, None, :], 0), 2
    )
    return document, places[None] - doc_begin, (pad_mask == 0) | is_first


def cross_section(base, cot_rows, embed_pick, allowed, segment_embed, weights):
    cross_in = weights[0]
    tail_weights = weights[1:]
    rows, width = base.shape
    slots = rows // SLOT_SEGS
    cross_input = base + exact_dot(embed_pick, segment_embed)
    cross_low = cross_input.astype(jnp.bfloat16)
    packed = matmul(cross_low, cross_in).astype(jnp.bfloat16)
    queries = to_heads(packed[:, :width], slots)
    keys = to_heads(packed[:, width : 2 * width], slots)
    values = to_heads(packed[:, 2 * width :], slots)
    probs, probs_low, attended = attend_forward(queries, keys, values, allowed)
    result, state = tail_forward(cross_input, attended.reshape(rows, width), tail_weights)
    grad_in, grad_att, tail_grads, factors = tail_backward_factors(state, tail_weights, cot_rows)
    grad_packed = attend_backward(probs, probs_low, queries, keys, values, to_heads(grad_att, slots), rows)
    grad_input = grad_in + back_product(grad_packed, cross_in)
    return result, grad_input, (cross_low, grad_packed) + factors, tail_grads


def attend_backward(probs, probs_low, queries, keys, values, grad_att, rows):
    scores_grad = score_grads(probs, grad_att, values)
    grad_query = jnp.einsum("bhqk,bkhe->bqhe", scores_grad, keys, preferred_element_type=jnp.float32) * HD ** (-0.5)
    grad_key = jnp.einsum("bhqk,bqhe->bkhe", scores_grad, queries, preferred_element_type=jnp.float32) * HD ** (-0.5)
    grad_value = jnp.einsum("bhqk,bqhe->bkhe", probs_low, grad_att, preferred_element_type=jnp.float32)
    return jnp.concatenate([g.reshape(rows, H * HD) for g in (grad_query, grad_key, grad_value)], 1).astype(jnp.bfloat16)


def tail_backward_factors(state, weights, upstream):
    attn_proj, norm_attn, ffn_up, ffn_down, norm_ffn = weights
    attended, first_state, first_low, pre_act, hidden, second_state = state
    grad_second, grad_norm_ffn = norm_backward(second_state, norm_ffn, upstream)
    grad_out_low = grad_second.astype(jnp.bfloat16)
    spare, gelu_back = jax.vjp(partial(jax.nn.gelu, approximate=False), pre_act)
    grad_pre = gelu_back(back_product(grad_out_low, ffn_down))[0].astype(jnp.bfloat16)
    grad_first = grad_second + back_product(grad_pre, ffn_up)
    grad_residual, grad_norm_attn = norm_backward(first_state, norm_attn, grad_first)
    grad_proj_out = grad_residual.astype(jnp.bfloat16)
    grad_att = back_product(grad_proj_out, attn_proj).astype(jnp.bfloat16)
    factors = (attended, grad_proj_out, first_low, grad_pre, hidden, grad_out_low)
    return grad_residual, grad_att, (grad_norm_attn, grad_norm_ffn), factors


def reduce_weights(grads, groups, members):
    parts = [lax.psum_scatter(g.astype(jnp.bfloat16), "seg", scatter_dimension=0, tiled=True) for g in grads]
    flat = [p.reshape(p.shape[0], groups, -1).transpose(1, 0, 2).reshape(groups, -1) for p in parts]
    joined = lax.psum_scatter(jnp.concatenate(flat, 1), "dp", scatter_dimension=0, tiled=True)[0].astype(jnp.float32)
    outs, at = [], 0
    for p in parts:
        rows, columns = p.shape[0], p.shape[1] // groups
        outs.append(joined[at : at + rows * columns].reshape(rows, columns))
        at += rows * columns
    return outs


def on_device(
    tokens, doc_counts, pad_mask, attn_in, attn_proj, norm_attn, ffn_up, ffn_down, norm_ffn,
    segment_embed, cross_in, cross_proj, cross_norm_attn, cross_up, cross_down, cross_norm_ffn,
    cotangent,
):
    seg_count, seg_length, width = tokens.shape
    rows = seg_count * seg_length
    members, groups = lax.axis_size("seg"), lax.axis_size("dp")
    member, group = lax.axis_index("seg"), lax.axis_index("dp")
    device = group * members + member
    token_rows = tokens.reshape(rows, width)
    seg_weights = (attn_in, attn_proj, norm_attn, ffn_up, ffn_down, norm_ffn)
    cross_weights = (cross_in, cross_proj, cross_norm_attn, cross_up, cross_down, cross_norm_ffn)

    slot_of, place_of = row_places(groups, members, seg_count)
    order = np.argsort(slot_of * SLOT_SEGS + place_of)
    slots = pad_mask.shape[0]
    document, rank, key_ok = documents(doc_counts, pad_mask)
    allowed = (document[:, :, None] == document[:, None, :]) & key_ok[:, None, :]
    embed_pick = (
        rank.reshape(-1)[:, None] == jnp.arange(segment_embed.shape[0], dtype=jnp.int32)[None]
    ).astype(jnp.float32)

    cot_first = lax.all_gather(cotangent[:, 0, :], ("dp", "seg"), axis=0, tiled=True)[order]
    seg_result, seg_state = segment_forward(token_rows, seg_count, seg_weights)
    seg_cube = seg_result.reshape(seg_count, seg_length, width)
    base = lax.all_gather(seg_cube[:, 0, :], ("dp", "seg"), axis=0, tiled=True)[order]
    cross_result, cross_grad, factors, cross_gains = cross_section(
        base, cot_first.astype(jnp.float32), embed_pick, allowed[:, None], segment_embed, cross_weights
    )
    back = np.argsort(order)
    own = lambda a: lax.dynamic_slice_in_dim(a[back], device * seg_count, seg_count, 0)
    output = jnp.concatenate(
        [own(cross_result.astype(jnp.bfloat16))[:, None, :], seg_cube[:, 1:, :].astype(jnp.bfloat16)], 1
    )

    def share(left, right):
        r, c = left.shape[1] // members, right.shape[1] // groups
        return outer_sum(
            lax.dynamic_slice_in_dim(left, member * r, r, 1), lax.dynamic_slice_in_dim(right, group * c, c, 1)
        )

    cross_low, cross_packed, cross_att, cross_proj_out, cross_first, cross_pre, cross_hidden, cross_out = factors
    grad_cross_in = share(cross_low, cross_packed)
    grad_cross_proj = share(cross_att, cross_proj_out)
    grad_cross_up = share(cross_first, cross_pre)
    grad_cross_down = share(cross_hidden, cross_out)
    er, ec = segment_embed.shape[0] // groups, width // members
    grad_embed = lax.dot_general(
        lax.dynamic_slice_in_dim(embed_pick, group * er, er, 1),
        lax.dynamic_slice_in_dim(cross_grad, member * ec, ec, 1),
        (((0,), (0,)), ((), ())), precision=lax.Precision.HIGHEST,
    )
    piece = lambda g: lax.dynamic_slice_in_dim(g, member * ec, ec, 0)

    upstream = cotangent.astype(jnp.float32)
    seg_upstream = jnp.concatenate([own(cross_grad)[:, None, :], upstream[:, 1:, :]], 1).reshape(rows, width)
    queries, key_heads, values, attn_probs, probs_low, tail_state = seg_state
    grad_residual, grad_att, seg_tail_grads, spare = tail_backward(tail_state, seg_weights[1:], seg_upstream)
    grad_packed = attend_backward(
        attn_probs, probs_low, queries, key_heads, values, to_heads(grad_att, seg_count), rows
    )
    grad_attn_in = outer_sum(token_rows, grad_packed)
    token_grad = (grad_residual + back_product(grad_packed, attn_in)).astype(jnp.bfloat16).reshape(tokens.shape)
    grad_attn_proj, grad_norm_attn, grad_ffn_up, grad_ffn_down, grad_norm_ffn = seg_tail_grads
    total_in, total_proj, total_up, total_down = reduce_weights(
        (grad_attn_in, grad_attn_proj, grad_ffn_up, grad_ffn_down), groups, members
    )
    gains = lax.psum(jnp.concatenate([grad_norm_attn, grad_norm_ffn]), ("dp", "seg"))
    return (
        output, token_grad, total_in, total_proj, piece(gains[:width]), total_up, total_down,
        piece(gains[width:]), grad_embed, grad_cross_in, grad_cross_proj, piece(cross_gains[0]),
        grad_cross_up, grad_cross_down, piece(cross_gains[1]),
    )


def solution(mesh):
    placed = (
        P(("dp", "seg"), None, None),
        P(),
        P(),
        P(),
        P(),
        P(),
        P(),
        P(),
        P(),
        P(),
        P(),
        P(),
        P(),
        P(),
        P(),
        P(),
        P(("dp", "seg"), None, None),
    )
    return jax.shard_map(
        on_device,
        mesh=mesh,
        in_specs=placed,
        out_specs=(
            P(("dp", "seg"), None, None),
            P(("dp", "seg"), None, None),
            P("seg", "dp"),
            P("seg", "dp"),
            P("seg"),
            P("seg", "dp"),
            P("seg", "dp"),
            P("seg"),
            P("dp", "seg"),
            P("seg", "dp"),
            P("seg", "dp"),
            P("seg"),
            P("seg", "dp"),
            P("seg", "dp"),
            P("seg"),
        ),
        check_vma=False,
    )
```

time: 1100 us -> 574 us (0.52)
  waiting for transfers between devices: 703 us -> 118 us
  blocking collectives: 95 us -> 135 us
  local copies, waits for them, and re-layouts: 101 us -> 127 us
    reduce_scatter x10 -> x3, waiting for transfers between devices: 537 us -> 83.3 us  [reduce_weights(): lax.psum_scatter(g.astype(jnp.bfloat16), 'seg', scatter_dimension=0, tile...]
    unnamed x24 -> x7, waiting for transfers between devices: 166 us -> 35.2 us
    all_gather x1 -> x2, blocking collectives: 16.8 us -> 95.1 us  [the longest x1 50.2 us: on_device(): lax.all_gather(cotangent[:, 0, :], ('dp', 'seg'), axis=0, tiled=True)[order]]
    unnamed x3 -> x0, blocking collectives: 67.4 us -> none
    psum x1, blocking collectives: 10.8 us -> 40.4 us  [on_device(): lax.psum(jnp.concatenate([grad_norm_attn, grad_norm_ffn]), ('dp', 'seg'))]
    unnamed x180 -> x166, local copies, waits for them, and re-layouts: 51.4 us -> 26.5 us
    reshape x4 -> x11, local copies, waits for them, and re-layouts: 6.16 us -> 23.2 us  [the longest x7 15 us: reduce_weights(): p.reshape(p.shape[0], groups, -1).transpose(1, 0, 2).reshape(groups, -1)]
    convert_element_type x13 -> x4, other arithmetic: 22.3 us -> 5.84 us  [the longest x1 2.84 us: reduce_weights(): lax.psum_scatter(jnp.concatenate(flat, 1), 'dp', scatter_dimension=0, til...]
  transfers between devices with their start and end apart: 17 -> 5, of which waited for: 13 -> 3; matrix products, arithmetic and copies ran while one was open for 12% -> 16% of each run, Pallas kernels for 0% -> 0%
where the time goes in v1:
time: 574 us; the launch traced here: 567 us
  blocking collectives  135 us (24%)
  matrix products  132 us (23%)
  local copies, waits for them, and re-layouts  127 us (22%)
  waiting for transfers between devices  118 us (21%)
  other arithmetic  39.2 us (7%)
  between operations  15 us (3%)
    reduce_scatter x3, waiting for transfers between devices, reduce_weights(): lax.psum_scatter(g.astype(jnp.bfloat16), 'seg', scatter_dimension=0, tile...  83.3 us
    all_gather x1, blocking collectives, on_device(): lax.all_gather(cotangent[:, 0, :], ('dp', 'seg'), axis=0, tiled=True)[order]  50.2 us
    all_gather x1, blocking collectives, on_device(): lax.all_gather(seg_cube[:, 0, :], ('dp', 'seg'), axis=0, tiled=True)[order]  44.8 us
    psum x1, blocking collectives, on_device(): lax.psum(jnp.concatenate([grad_norm_attn, grad_norm_ffn]), ('dp', 'seg'))  40.4 us
    dot_general x8, matrix products, matmul(): return jnp.dot(former, latter, preferred_element_type=jnp.float32)  40.2 us
    dot_general x8, matrix products, back_product(): lax.dot_general(gradient, weight, (((1,), (1,)), ((), ())), preferred_ele...  38.1 us
    unnamed x7, waiting for transfers between devices  35.2 us
    dot_general x8, matrix products, outer_sum(): lax.dot_general(former, latter, (((0,), (0,)), ((), ())), preferred_eleme...  28 us
  transfers between devices with their start and end apart: 5, of which 3 were waited for; matrix products, arithmetic and copies ran while one was open for 16% of the time, Pallas kernels for 0%

profile of v1, /device:TPU:0, one launch (start us, length us, event | category | flops | bytes accessed | tf_op | source)
XLA Modules:
  0.0 567.5 jit_solution(9447778987128580068)
XLA Ops:
  10.2 3.1 convolution_convert_fusion.3
  14.8 2.3 copy.188
  17.1 2.4 reshape.262
  19.5 2.3 copy.189
  21.8 2.5 reshape.263
  24.3 2.0 fusion.46
  26.3 3.0 fusion.107
  29.3 2.3 copy.187
  31.6 2.4 reshape.261
  34.0 2.7 fusion.23
  40.5 19.5 %multiply_convert_fusion = (bf16[512,3072]{1,0:T(8,128)(2,1)S(1)}, f32[512,3072]{1,0:T(8,128)}, f32[512,3072]{1,0:T(8,128)}) fusion(bf16[768,3072]{1,0:T(8,128)(2,1)} %param.29, f32[512,768]{1,0:T(8,128)S(1)} %get-tuple-element.107, f32[768]{0:T(1024)S(1)} %copy-done.60, f32[512]{0:T(512)S(1)} %add_rsqrt_fusion.1, f32[512]{0:T(512)S(1)} %broadcast_multiply_fusion.4), kind=kOutput, calls=%fused_computation.9 | convolution fusion | flops 2519728128 | bytes 22027264 | tf_op jit(solution)/shard_map/dot_general | solution.py:19
  60.1 2.7 fusion.109
  65.3 44.8 %all-gather = f32[128,1,768]{2,1,0:T(1,128)S(1)} all-gather(f32[4,1,768]{2,1,0:T(1,128)S(1)} %slice.110), channel_id=2, replica_groups=mesh['dp'=4,'seg'=8] {'dp','seg'}, dimensions={0}, use_global_device_ids=true | all-gather | bytes 405504 | tf_op jit(solution)/shard_map/all_gather | solution.py:228
  113.7 2.8 gather_fusion
  116.5 2.2 fusion.110
  118.7 2.7 convolution_convert_fusion.4
  122.3 2.1 reshape.267
  124.3 2.1 reshape.268
  131.3 2.1 reshape.266
  133.4 2.7 fusion.29
  136.1 2.0 copy.201
  138.1 2.1 reshape.269
  140.2 2.0 fusion.112
  142.6 8.3 %multiply_convert_fusion.4 = (bf16[128,3072]{1,0:T(8,128)(2,1)S(1)}, f32[128,3072]{1,0:T(8,128)}, f32[128,3072]{1,0:T(8,128)}) fusion(bf16[128,768]{1,0:T(8,128)(2,1)S(1)} %multiply_convert_fusion.8, bf16[768,3072]{1,0:T(8,128)(2,1)} %param.36), kind=kOutput, calls=%fused_computation.52 | convolution fusion | flops 629538816 | bytes 8847360 | tf_op jit(solution)/shard_map/dot_general | solution.py:19
  154.2 50.2 %all-gather.1 = bf16[128,1,768]{2,1,0:T(2,128)(2,1)S(1)} all-gather(bf16[4,1,768]{2,1,0:T(2,128)(2,1)S(1)} %slice.82), channel_id=3, replica_groups=mesh['dp'=4,'seg'=8] {'dp','seg'}, dimensions={0}, use_global_device_ids=true | all-gather | bytes 202752 | tf_op jit(solution)/shard_map/all_gather | solution.py:225
  205.1 2.7 gather_fusion.2
  207.8 2.0 fusion.56
  211.8 4.8 add_convert_fusion.2
  216.7 5.1 multiply_reduce_fusion.10
  224.6 2.1 reshape.270
  226.7 2.7 fusion.30
  236.7 2.1 reshape.273
  240.8 2.1 reshape.272
  244.8 2.1 reshape.271
  251.8 4.3 convolution_add_fusion.3
  256.0 2.7 gather_fusion.3
  263.1 9.2 %add_convert_fusion = bf16[512,3072]{1,0:T(8,128)(2,1)} fusion(f32[512,3072]{1,0:T(8,128)} %get-tuple-element.93, f32[512,3072]{1,0:T(8,128)} %get-tuple-element.108, bf16[3072,768]{1,0:T(8,128)(2,1)S(1)} %bitcast.151, f32[512,768]{1,0:T(8,128)S(1)} %subtract_multiply_fusion.1), kind=kOutput, calls=%fused_computation.8 | convolution fusion | flops 2438332416 | bytes 22020096 | tf_op jit(solution)/shard_map/dot_general | solution.py:33
  272.3 5.6 multiply_reduce_fusion.2
  281.5 3.4 convolution_convert_fusion.6
  284.9 2.3 copy.213
  287.2 2.8 reshape.275
  290.1 3.4 fusion.24
  300.9 3.8 fusion.8
  304.7 5.8 %copy.236 = bf16[768,2304]{1,0:T(8,128)(2,1)} copy(bf16[768,2304]{0,1:T(8,128)(2,1)} %fusion.8) | data formatting | bytes 7077888
  310.6 7.2 %convolution_convert_fusion = bf16[3072,768]{1,0:T(8,128)(2,1)} fusion(bf16[512,3072]{1,0:T(8,128)(2,1)} %copy-done.69, f32[512,768]{1,0:T(8,128)} %copy-done.23), kind=kOutput, calls=%fused_computation.23 | convolution fusion | flops 2418671616 | bytes 9437184 | tf_op jit(solution)/shard_map/dot_general | solution.py:27
  318.0 7.4 %convolution_convert_fusion.1 = bf16[768,3072]{1,0:T(8,128)(2,1)} fusion(bf16[512,3072]{1,0:T(8,128)(2,1)} %add_convert_fusion, f32[512,768]{1,0:T(8,128)} %copy-done.12, f32[768]{0:T(1024)S(1)} %copy-done.61, f32[512]{0:T(512)S(1)} %copy-done.50, f32[512]{0:T(512)S(1)} %copy-done.44), kind=kOutput, calls=%fused_computation.24 | convolution fusion | flops 2419851264 | bytes 9444352 | tf_op jit(solution)/shard_map/dot_general | solution.py:27
  326.1 40.4 %psum.7 = f32[1536]{0:T(1024)S(1)} all-reduce(f32[1536]{0:T(1024)S(1)} %pad_maximum_fusion.3), channel_id=1, replica_groups=mesh['dp'=4,'seg'=8] {'dp','seg'}, use_global_device_ids=true, to_apply=%region_33.34 | all-reduce | flops 1536 | bytes 12288 | tf_op jit(solution)/shard_map/psum | solution.py:270
  371.7 2.1 copy.237
  373.8 2.1 copy.225
  375.9 2.4 reshape.281
  378.3 34.9 %reduce-scatter.11.cloned.1.call-done = bf16[384,768]{1,0:T(8,128)(2,1)} async-done(((bf16[3072,768]{1,0:T(8,128)(2,1)}), bf16[384,768]{1,0:T(8,128)(2,1)}) %reduce-scatter.11.cloned.1.call-update) | async-done | bytes 589840 | tf_op jit(solution)/shard_map/reduce_scatter | solution.py:191
  413.2 2.1 copy.227
  415.3 2.2 copy.228
  417.5 2.8 reshape.287
  420.3 48.4 %reduce-scatter.9.cloned.1.call-done = bf16[96,3072]{1,0:T(8,128)(2,1)} async-done(((bf16[768,3072]{1,0:T(8,128)(2,1)}), bf16[96,3072]{1,0:T(8,128)(2,1)}) %reduce-scatter.9.cloned.1.call-update) | async-done | bytes 589840 | tf_op jit(solution)/shard_map/reduce_scatter | solution.py:191
  468.7 2.5 reshape.284
  471.2 6.5 %pad_maximum_fusion = bf16[4,221184]{1,0:T(4,128)(2,1)} fusion(bf16[4,73728]{1,0:T(4,128)(2,1)} %reshape.287, bf16[4,73728]{1,0:T(4,128)(2,1)} %bitcast.143, bf16[4,18432]{1,0:T(4,128)(2,1)} %reshape.283, bf16[4,55296]{1,0:T(4,128)(2,1)} %reshape.281), kind=kLoop, calls=%fused_computation.35 | loop fusion | flops 7077888 | bytes 3538944 | tf_op jit(solution)/shard_map/concatenate | solution.py:193
  478.3 2.4 slice.130
  483.8 2.7 gather_fusion.1
  500.7 4.6 add_convert_fusion.1
  505.3 35.1 %all-reduce.3.cloned.1.call-done = bf16[4,221184]{1,0:T(4,128)(2,1)} async-done(((bf16[4,221184]{1,0:T(4,128)(2,1)}), bf16[4,221184]{1,0:T(4,128)(2,1)}) %all-reduce.3.cloned.1.call-update) | async-done | bytes 1769488
  540.4 2.8 dynamic-slice_convert_fusion
  550.8 3.5 fusion.64
  556.0 3.0 fusion.74
  (274 shorter events, 95.3 us)
Async XLA Ops:
  7.2 3.0 copy-start
  7.2 359.3 %reduce-scatter.7.cloned.1.call-start = ((), (), s32[]{:S(2)}) async-start(), calls=%async_computation.4 | async-start | bytes 1327104 | tf_op jit(solution)/shard_map/reduce_scatter | solution.py:191
  34.0 3.4 copy-start.66
  38.0 22.1 %slice-start.2 = ((s8[4718592]{0:T(1024)(128)(4,1)}), s8[4194304]{0:T(1024)(128)(4,1)S(1)}, s32[]{:S(2)}) async-start(s8[4718592]{0:T(1024)(128)(4,1)} %bitcast.148), calls=%async_computation.11 | async-start | bytes 8388608
  38.9 21.1 %copy-start.12 = (f32[512,768]{1,0:T(8,128)}, f32[512,768]{1,0:T(8,128)S(1)}, u32[]{:S(2)}) copy-start(f32[512,768]{1,0:T(8,128)S(1)} %get-tuple-element.107) | copy-start | bytes 4718596
  39.0 21.1 %copy-start.43 = (f32[512]{0:T(512)}, f32[512]{0:T(512)S(1)}, u32[]{:S(2)}) copy-start(f32[512]{0:T(512)S(1)} %broadcast_multiply_fusion.4) | copy-start | bytes 6148
  40.5 19.5 %copy-start.49 = (f32[512]{0:T(512)}, f32[512]{0:T(512)S(1)}, u32[]{:S(2)}) copy-start(f32[512]{0:T(512)S(1)} %add_rsqrt_fusion.1) | copy-start | bytes 6148
  40.5 19.6 %slice-start.3 = ((s8[4718592]{0:T(1024)(128)(4,1)}), s8[524288]{0:T(1024)(128)(4,1)S(1)}, s32[]{:S(2)}) async-start(s8[4718592]{0:T(1024)(128)(4,1)} %bitcast.148), calls=%async_computation.12 | async-start | bytes 1048576
  60.0 2.8 copy-start.69
  63.6 47.3 %copy-start.64 = (s32[128]{0:T(128)S(1)}, s32[128]{0:T(128)}, u32[]{:S(2)}) copy-start(s32[128]{0:T(128)} %constant.39) | copy-start | bytes 1540
  63.6 47.9 %copy-start.46 = (s32[4,6]{0,1:T(8,128)S(1)}, s32[4,6]{0,1:T(8,128)}, u32[]{:S(2)}) copy-start(s32[4,6]{0,1:T(8,128)} %copy.195) | copy-start | bytes 292
  113.7 2.8 copy-start.56
  118.7 2.7 copy-start.27
  121.4 5.0 copy-start.62
  138.1 4.3 copy-start.38
  140.2 10.8 %slice-start = ((s8[4718592]{0:T(1024)(128)(4,1)}), s8[4194304]{0:T(1024)(128)(4,1)S(1)}, s32[]{:S(2)}) async-start(s8[4718592]{0:T(1024)(128)(4,1)} %bitcast.134), calls=%async_computation.9 | async-start | bytes 8388608
  142.1 8.7 %copy-start.3 = (f32[128,768]{1,0:T(8,128)}, f32[128,768]{1,0:T(8,128)S(1)}, u32[]{:S(2)}) copy-start(f32[128,768]{1,0:T(8,128)S(1)} %get-tuple-element.116) | copy-start | bytes 1179652
  142.2 8.7 %copy-start.47 = (f32[128]{0:T(128)}, f32[128]{0:T(128)S(1)}, u32[]{:S(2)}) copy-start(f32[128]{0:T(128)S(1)} %broadcast_multiply_fusion.10) | copy-start | bytes 1540
  142.4 8.5 %copy-start.51 = (f32[128]{0:T(128)}, f32[128]{0:T(128)S(1)}, u32[]{:S(2)}) copy-start(f32[128]{0:T(128)S(1)} %add_rsqrt_fusion.3) | copy-start | bytes 1540
  142.5 8.3 %copy-start.34 = (bf16[128,768]{1,0:T(8,128)(2,1)}, bf16[128,768]{1,0:T(8,128)(2,1)S(1)}, u32[]{:S(2)}) copy-start(bf16[128,768]{1,0:T(8,128)(2,1)S(1)} %multiply_convert_fusion.8) | copy-start | bytes 589828
  142.5 8.4 %slice-start.1 = ((s8[4718592]{0:T(1024)(128)(4,1)}), s8[524288]{0:T(1024)(128)(4,1)S(1)}, s32[]{:S(2)}) async-start(s8[4718592]{0:T(1024)(128)(4,1)} %bitcast.134), calls=%async_computation.10 | async-start | bytes 1048576
  152.6 55.2 %copy-start.40 = (f32[768]{0:T(1024)S(1)}, f32[768]{0:T(1024)}, u32[]{:S(2)}) copy-start(f32[768]{0:T(1024)} %param.38) | copy-start | bytes 9220
  207.8 3.9 copy-start.68
  211.8 4.9 copy-start.33
  211.8 4.9 copy-start.4
  211.8 4.9 copy-start.7
  211.8 4.9 copy-start.20
  211.8 4.9 copy-start.48
  211.8 4.9 copy-start.52
  211.8 4.9 copy-start.54
  211.8 4.9 copy-start.58
  216.7 5.1 copy-start.24
  229.4 1.9 copy-start.19
  229.4 1.9 copy-start.37
  231.3 2.0 copy-start.22
  232.3 2.1 copy-start.28
  233.3 2.4 copy-start.32
  240.8 7.7 %copy-start.63 = (s32[128]{0:T(128)S(1)}, s32[128]{0:T(128)}, u32[]{:S(2)}) copy-start(s32[128]{0:T(128)} %constant.40) | copy-start | bytes 1540
  248.5 7.5 %copy-start.55 = (s32[1024]{0:T(1024)}, s32[1024]{0:T(1024)S(1)}, u32[]{:S(2)}) copy-start(s32[1024]{0:T(1024)S(1)} %pad_clamp_fusion) | copy-start | bytes 12292
  259.5 1.9 copy-start.2
  259.5 1.9 copy-start.42
  259.5 3.5 slice-start.4
  261.4 1.6 slice-start.5
  262.6 9.7 %slice-start.6 = ((s8[4718592]{0:T(1024)(128)(4,1)}), s8[4194304]{0:T(1024)(128)(4,1)S(1)}, s32[]{:S(2)}) async-start(s8[4718592]{0:T(1024)(128)(4,1)} %bitcast.152), calls=%async_computation.15 | async-start | bytes 8388608
  263.0 9.3 %copy-start.23 = (f32[512,768]{1,0:T(8,128)}, f32[512,768]{1,0:T(8,128)S(1)}, u32[]{:S(2)}) copy-start(f32[512,768]{1,0:T(8,128)S(1)} %subtract_multiply_fusion.1) | copy-start | bytes 4718596
  263.1 9.2 %copy-start.13 = (f32[512,768]{1,0:T(8,128)S(1)}, f32[512,768]{1,0:T(8,128)}, u32[]{:S(2)}) copy-start(f32[512,768]{1,0:T(8,128)} %copy-done.12) | copy-start | bytes 4718596
  263.1 9.2 %copy-start.44 = (f32[512]{0:T(512)S(1)}, f32[512]{0:T(512)}, u32[]{:S(2)}) copy-start(f32[512]{0:T(512)} %copy-done.43) | copy-start | bytes 6148
  263.1 9.2 %copy-start.50 = (f32[512]{0:T(512)S(1)}, f32[512]{0:T(512)}, u32[]{:S(2)}) copy-start(f32[512]{0:T(512)} %copy-done.49) | copy-start | bytes 6148
  263.1 9.2 %copy-start.61 = (f32[768]{0:T(1024)S(1)}, f32[768]{0:T(1024)}, u32[]{:S(2)}) copy-start(f32[768]{0:T(1024)} %param.28) | copy-start | bytes 9220
  263.1 9.2 %slice-start.7 = ((s8[4718592]{0:T(1024)(128)(4,1)}), s8[524288]{0:T(1024)(128)(4,1)S(1)}, s32[]{:S(2)}) async-start(s8[4718592]{0:T(1024)(128)(4,1)} %bitcast.152), calls=%async_computation.16 | async-start | bytes 1048576
  277.9 1.7 copy-start.17
  281.4 90.3 %reduce-scatter.13.cloned.1.call-start = ((), (), s32[]{:S(2)}) async-start(), calls=%async_computation.7 | async-start | bytes 3981312
  290.0 3.5 copy-start.5
  290.0 3.5 copy-start.29
  290.0 3.6 copy-start.31
  290.0 3.6 copy-start.36
  296.2 1.8 copy-start.9
  299.3 1.7 copy-start.67
  310.5 102.7 %reduce-scatter.11.cloned.1.call-start = ((), (), s32[]{:S(2)}) async-start(), calls=%async_computation.6 | async-start | bytes 5308416 | tf_op jit(solution)/shard_map/reduce_scatter | solution.py:191
  317.8 150.9 %reduce-scatter.9.cloned.1.call-start = ((), (), s32[]{:S(2)}) async-start(), calls=%async_computation.5 | async-start | bytes 5308416 | tf_op jit(solution)/shard_map/reduce_scatter | solution.py:191
  325.5 214.9 %all-reduce.3.cloned.1.call-start = ((), (), s32[]{:S(2)}) async-start(), calls=%async_computation.8 | async-start | bytes 3538944
  478.3 11.5 %copy-start.57 = (s32[128]{0:T(128)S(1)}, s32[128]{0:T(128)}, u32[]{:S(2)}) copy-start(s32[128]{0:T(128)} %sub.135) | copy-start | bytes 1540
  489.8 9.8 %copy-start.18 = (bf16[4,127,768]{2,1,0:T(8,128)(2,1)S(1)}, bf16[4,127,768]{2,1,0:T(8,128)(2,1)}, u32[]{:S(2)}) copy-start(bf16[4,127,768]{2,1,0:T(8,128)(2,1)} %slice.130) | copy-start | bytes 2340868
  491.8 8.9 %copy-start.11 = (f32[512,768]{1,0:T(8,128)S(1)}, f32[512,768]{1,0:T(8,128)}, u32[]{:S(2)}) copy-start(f32[512,768]{1,0:T(8,128)} %copy-done.10) | copy-start | bytes 4718596
  (19 other events, 20.6 us)
Sparse Core Ops, SparseCore 0:
  281.6 30.3 reduce-scatter.6
  314.3 42.8 reduce-scatter.12
  359.4 53.7 reduce-scatter.10
  415.3 53.3 reduce-scatter.8
  477.8 62.5 all-reduce.2

commit v2 on v1

--- a/solution.py
+++ b/solution.py
@@ -3,6 +3,8 @@
 import jax
 import jax.numpy as jnp
 import numpy as np
+from jax.experimental import pallas as pl
+from jax.experimental.pallas import tpu as pltpu
 from jax import lax
 from jax.sharding import PartitionSpec as P
 
@@ -199,7 +201,7 @@
     return outs
 
 
-def on_device(
+def any_mesh(
     tokens, doc_counts, pad_mask, attn_in, attn_proj, norm_attn, ffn_up, ffn_down, norm_ffn,
     segment_embed, cross_in, cross_proj, cross_norm_attn, cross_up, cross_down, cross_norm_ffn,
     cotangent,
@@ -275,7 +277,642 @@
     )
 
 
+BF16, F32 = jnp.bfloat16, jnp.float32
+QUAD = 4 * HD
+ERFC = (0.23192104, 0.16183046, 0.46825631, -0.37088501, 0.70913273, -0.20025555)
+
+def nn(a, b): return jnp.dot(a, b, preferred_element_type=F32)
+def nt(a, b): return lax.dot_general(a, b, (((1,), (1,)), ((), ())), preferred_element_type=F32)
+def tn(a, b): return lax.dot_general(a, b, (((0,), (0,)), ((), ())), preferred_element_type=F32)
+
+def gelu_pair(v):
+    size = jnp.abs(v)
+    t = 1.0 / (1.0 + (0.4 * 0.5 ** 0.5) * size)
+    bell = jnp.exp(-0.5 * (v * v))
+    poly = F32(0.5 * ERFC[5])
+    for c in ERFC[4::-1]:
+        poly = poly * t + F32(0.5 * c)
+    tail = poly * t * bell
+    cdf = jnp.where(v >= 0, 1.0 - tail, tail)
+    scaled = v * cdf
+    return scaled, cdf + v * (bell * F32((2 * np.pi) ** -0.5))
+
+def mean(v): return jnp.mean(v, -1, keepdims=True)
+
+def unit(total):
+    middle = total - mean(total)
+    inverse = lax.rsqrt(mean(middle * middle) + EPSILON)
+    return middle * inverse, inverse
+
+def lanes(start, size):
+    return pl.ds(pl.multiple_of(start, 128), size)
+
+def head_mask(rows):
+    lane = lax.broadcasted_iota(jnp.int32, (rows, QUAD), 1)
+    return [lane // HD == h for h in range(4)]
+
+def stacked(v, masks):
+    zero = jnp.zeros_like(v)
+    return jnp.concatenate([jnp.where(m, v, zero) for m in masks], 0)
+
+def picked(v, masks):
+    n = v.shape[0] // 4
+    out = v[3 * n :]
+    for h in (2, 1, 0):
+        out = jnp.where(masks[h], v[h * n : (h + 1) * n], out)
+    return out
+
+def forward_kernel(segs, x, w_in, w_proj, w_up, w_down, ga, gf,
+                   qkv_o, probs_o, att_o, unit1_o, unit2_o, inv_o, hidden_o, slope_o, out_o, row_o,
+                   win, wproj, wup, wdown, qkv, probs, att, unit1, unit2, inv, hidden, slope, out, acc, low, in_sem, out_sem):
+    rows, width = x.shape
+    length = rows // segs
+    loads = [pltpu.make_async_copy(a, b, in_sem.at[k]) for k, (a, b) in enumerate(((w_in, win), (w_proj, wproj), (w_up, wup), (w_down, wdown)))]
+    for load in loads: load.start()
+    saves = []
+    def save(a, b):
+        copy = pltpu.make_async_copy(a, b, out_sem.at[len(saves)])
+        copy.start(); saves.append(copy)
+    loads[0].wait()
+    def project(n, c):
+        s = lanes(n * width, width)
+        qkv[:, s] = nn(x[...], win[:, s]).astype(BF16)
+        return c
+    lax.fori_loop(0, 3, project, 0)
+    save(qkv, qkv_o)
+    masks = head_mask(length)
+    def attend(n, c):
+        seg, quad = n // 3, n % 3
+        r = pl.ds(pl.multiple_of(seg * length, length), length)
+        q = stacked(qkv[r, lanes(quad * QUAD, QUAD)], masks)
+        scores = nt(q, qkv[r, lanes(width + quad * QUAD, QUAD)]) * HD ** -0.5
+        e = jnp.exp(scores - jnp.max(scores, -1, keepdims=True))
+        p = e / jnp.sum(e, -1, keepdims=True)
+        probs[n] = p
+        o = nn(p.astype(BF16), qkv[r, lanes(2 * width + quad * QUAD, QUAD)])
+        att[r, lanes(quad * QUAD, QUAD)] = picked(o, masks).astype(BF16)
+        return c
+    lax.fori_loop(0, 3 * segs, attend, 0)
+    save(probs, probs_o); save(att, att_o)
+    loads[1].wait()
+    acc[...] = nn(att[...], wproj[...])
+    def first(n, c):
+        r = pl.ds(pl.multiple_of(n * length, length), length)
+        u, i = unit(x[r, :].astype(F32) + acc[r, :])
+        unit1[r, :] = u
+        inv[0, r, :] = jnp.broadcast_to(i, (length, 128))
+        f = u * ga[...]
+        acc[r, :] = f
+        low[r, :] = f.astype(BF16)
+        return c
+    lax.fori_loop(0, segs, first, 0)
+    save(unit1, unit1_o)
+    loads[2].wait()
+    tile = 512
+    def up(n, c):
+        s = lanes(n * tile, tile)
+        h, g = gelu_pair(nn(low[...], wup[:, s]))
+        hidden[:, s] = h.astype(BF16)
+        slope[:, s] = g.astype(BF16)
+        return c
+    lax.fori_loop(0, wup.shape[1] // tile, up, 0)
+    save(hidden, hidden_o); save(slope, slope_o)
+    loads[3].wait()
+    def down(n, c):
+        s = lanes(n * QUAD, QUAD)
+        acc[:, s] += nn(hidden[...], wdown[:, s])
+        return c
+    lax.fori_loop(0, width // QUAD, down, 0)
+    def second(n, c):
+        r = pl.ds(pl.multiple_of(n * length, length), length)
+        u, i = unit(acc[r, :])
+        unit2[r, :] = u
+        inv[1, r, :] = jnp.broadcast_to(i, (length, 128))
+        o = u * gf[...]
+        out[r, :] = o.astype(BF16)
+        row_o[pl.ds(n, 1), :] = o[:1]
+        return c
+    lax.fori_loop(0, segs, second, 0)
+    save(unit2, unit2_o); save(inv, inv_o); save(out, out_o)
+    for copy in saves: copy.wait()
+
+ANY = pl.BlockSpec(memory_space=pl.ANY)
+VM = pl.BlockSpec(memory_space=pltpu.VMEM)
+def sds(*a): return jax.ShapeDtypeStruct(*a)
+
+def forward(x, segs, weights):
+    w_in, w_proj, ga, w_up, w_down, gf = weights
+    rows, width = x.shape
+    ff = w_up.shape[1]
+    length = rows // segs
+    saved = [((rows, 3 * width), BF16), ((3 * segs, 4 * length, length), F32), ((rows, width), BF16), ((rows, width), F32),
+             ((rows, width), F32), ((2, rows, 128), F32), ((rows, ff), BF16), ((rows, ff), BF16), ((rows, width), BF16)]
+    return pl.pallas_call(
+        partial(forward_kernel, segs),
+        out_shape=[sds(*s) for s in saved] + [sds((segs, width), F32)],
+        in_specs=[VM, ANY, ANY, ANY, ANY, VM, VM],
+        out_specs=[ANY] * 9 + [VM],
+        scratch_shapes=[pltpu.VMEM(w.shape, BF16) for w in (w_in, w_proj, w_up, w_down)]
+        + [pltpu.VMEM(*s) for s in saved]
+        + [pltpu.VMEM((rows, width), F32), pltpu.VMEM((rows, width), BF16), pltpu.SemaphoreType.DMA((4,)), pltpu.SemaphoreType.DMA((9,))],
+        compiler_params=pltpu.CompilerParams(vmem_limit_bytes=60 << 20),
+        name="segment_forward",
+    )(x, w_in, w_proj, w_up, w_down, ga.reshape(1, -1), gf.reshape(1, -1))
+
+NC = 12
+MESH = pl.DeviceIdType.MESH
+
+def spots():
+    dp, seg = lax.axis_index("dp"), lax.axis_index("seg")
+    return dp // 2, dp % 2, seg // 2, seg % 2
+
+def norm_back(u, i, up, gain):
+    s = up * gain
+    return i * (s - mean(s) - u * mean(s * u)), jnp.sum(up * u, 0, keepdims=True)
+
+def backward_body(segs, x, cot, crossed, win, wproj, wup, wdown, ga, gf, qkv, probs, att, unit1, unit2, inv, hidden, slope,
+                  low, dy, gains, g, ready, tick):
+    rows, width = x.shape
+    length = rows // segs
+    ff = wup.shape[1]
+    top = lax.broadcasted_iota(jnp.int32, (length, 1), 0) == 0
+
+    def put(chunk, y, v, core_rows=96):
+        v = v.astype(BF16)
+        for j in range(8):
+            z, core = j // 2, j % 2
+            h, zz = z // 2, z % 2
+            for half in range(2):
+                part = v[j * 96 + half * 48 : j * 96 + half * 48 + 48]
+                p, q = (half, y) if h == 0 else (y, half)
+                g[chunk, core, h, p, q, zz] = part
+
+    gains[...] = jnp.zeros_like(gains)
+    def second(n, c):
+        r = pl.ds(pl.multiple_of(n * length, length), length)
+        up = jnp.where(top, crossed[pl.ds(n, 1), :], cot[r, :].astype(F32))
+        d, gain = norm_back(unit2[r, :], inv[1, r, :1], up, gf[...])
+        gains[1:2, :] += gain
+        unit2[r, :] = d
+        dy[r, :] = d.astype(BF16)
+        low[r, :] = (unit1[r, :] * ga[...]).astype(BF16)
+        return c
+    ready("norms")
+    lax.fori_loop(0, segs, second, 0)
+    ready("hidden")
+    def down_grad(j, c):
+        v = tn(hidden[:, lanes(j * 384, 384)], dy[...]).astype(BF16)
+        z, core = j // 2, j % 2
+        h, zz = z // 2, z % 2
+        for chunk in range(4):
+            for half in range(2):
+                for y in range(2):
+                    part = v[chunk * 96 + half * 48 : chunk * 96 + half * 48 + 48, y * 384 : y * 384 + 384]
+                    p = half * (1 - h) + y * h
+                    q = y * (1 - h) + half * h
+                    g[chunk, core, h, p, q, zz] = part
+        return c
+    lax.fori_loop(0, 8, down_grad, 0)
+    tick("down")
+    ready("slope")
+    tile = 512
+    def pre_grad(n, c):
+        s = lanes(n * tile, tile)
+        slope[:, s] = (nt(dy[...], wdown[pl.ds(pl.multiple_of(n * tile, tile), tile), :]) * slope[:, s].astype(F32)).astype(BF16)
+        return c
+    lax.fori_loop(0, ff // tile, pre_grad, 0)
+    def up_grad(n, c):
+        chunk, y = n // 2, n % 2
+        put(4 + chunk, y, tn(low[...], slope[:, lanes(y * (ff // 2) + chunk * 384, 384)]))
+        return c
+    lax.fori_loop(0, 8, up_grad, 0)
+    tick("up")
+    def first_grad(n, c):
+        unit2[:, lanes(n * QUAD, QUAD)] += nt(slope[...], wup[pl.ds(pl.multiple_of(n * QUAD, QUAD), QUAD), :])
+        return c
+    lax.fori_loop(0, width // QUAD, first_grad, 0)
+    def first(n, c):
+        r = pl.ds(pl.multiple_of(n * length, length), length)
+        d, gain = norm_back(unit1[r, :], inv[0, r, :1], unit2[r, :], ga[...])
+        gains[0:1, :] += gain
+        unit1[r, :] = d
+        dy[r, :] = d.astype(BF16)
+        return c
+    lax.fori_loop(0, segs, first, 0)
+    tick("gains")
+    ready("att")
+    def proj_grad(y, c):
+        put(8, y, tn(att[...], dy[:, lanes(y * 384, 384)]))
+        return c
+    lax.fori_loop(0, 2, proj_grad, 0)
+    tick("proj")
+    att[...] = nt(dy[...], wproj[...]).astype(BF16)
+    masks = head_mask(length)
+    ready("qkv")
+    def attend(n, c):
+        seg, quad = n // 3, n % 3
+        r = pl.ds(pl.multiple_of(seg * length, length), length)
+        qs, ks, vs = (lanes(k * width + quad * QUAD, QUAD) for k in range(3))
+        da = stacked(att[r, lanes(quad * QUAD, QUAD)], masks)
+        q, k = stacked(qkv[r, qs], masks), qkv[r, ks]
+        p = probs[n]
+        dp = nt(da, qkv[r, vs])
+        ds = (p * (dp - jnp.sum(p * dp, -1, keepdims=True))).astype(BF16)
+        qkv[r, qs] = (picked(nn(ds, k), masks) * HD ** -0.5).astype(BF16)
+        qkv[r, ks] = (tn(ds, q) * HD ** -0.5).astype(BF16)
+        qkv[r, vs] = tn(p.astype(BF16), da).astype(BF16)
+        return c
+    lax.fori_loop(0, 3 * segs, attend, 0)
+    tick("attention")
+    def in_grad(n, c):
+        chunk, y = n // 2, n % 2
+        put(9 + chunk, y, tn(x[...], qkv[:, lanes(y * (3 * width // 2) + chunk * 384, 384)]))
+        return c
+    lax.fori_loop(0, 6, in_grad, 0)
+    tick("in")
+    def token(n, c):
+        s = lanes(n * QUAD, QUAD)
+        cot[:, s] = (unit1[:, s] + nt(qkv[...], win[pl.ds(pl.multiple_of(n * QUAD, QUAD), QUAD), :])).astype(BF16)
+        return c
+    lax.fori_loop(0, width // QUAD, token, 0)
+    tick("token")
+
+SAVED = ("qkv", "probs", "att", "unit1", "unit2", "inv", "hidden", "slope")
+
+def backward_kernel(segs, x, cot_h, crossed, w_in, w_proj, w_up, w_down, ga, gf, *rest):
+    saved_h, rest = rest[:8], rest[8:]
+    token_o, gains_o, g_o = rest[:3]
+    cot, win, wproj, wup, wdown = rest[3:8]
+    saved = rest[8:16]
+    low, dy, g, in_sem, out_sem = rest[16:]
+    by = dict(zip(SAVED, zip(saved_h, saved)))
+    pairs = [(cot_h, cot), by["unit2"], by["inv"], by["unit1"], by["hidden"], (w_down, wdown), by["slope"], (w_up, wup), by["att"],
+             (w_proj, wproj), by["qkv"], by["probs"], (w_in, win)]
+    copies = [pltpu.make_async_copy(a, b, in_sem.at[k]) for k, (a, b) in enumerate(pairs)]
+    for copy in copies: copy.start()
+    groups = {"norms": copies[:4], "hidden": copies[4:5], "slope": copies[5:8], "att": copies[8:10], "qkv": copies[10:]}
+    def ready(k):
+        for copy in groups[k]: copy.wait()
+    out = []
+    def tick(k):
+        if k == "in":
+            copy = pltpu.make_async_copy(g, g_o, out_sem.at[0]); copy.start(); out.append(copy)
+        if k == "token":
+            copy = pltpu.make_async_copy(cot, token_o, out_sem.at[1]); copy.start(); out.append(copy)
+    backward_body(segs, x, cot, crossed, win, wproj, wup, wdown, ga, gf, *saved, low, dy, gains_o, g, ready, tick)
+    for copy in out: copy.wait()
+
+def backward(x, cot, crossed, saved, segs, weights):
+    w_in, w_proj, ga, w_up, w_down, gf = weights
+    rows, width = x.shape
+    gs = (NC, 2, 2, 2, 2, 2, 48, 384)
+    return pl.pallas_call(
+        partial(backward_kernel, segs),
+        out_shape=[sds((rows, width), BF16), sds((2, width), F32), sds(gs, BF16)],
+        in_specs=[VM, ANY, VM, ANY, ANY, ANY, ANY, VM, VM] + [ANY] * 8,
+        out_specs=[ANY, VM, ANY],
+        scratch_shapes=[pltpu.VMEM((rows, width), BF16)] + [pltpu.VMEM(w.shape, BF16) for w in (w_in, w_proj, w_up, w_down)]
+        + [pltpu.VMEM(s.shape, s.dtype) for s in saved]
+        + [pltpu.VMEM((rows, width), BF16), pltpu.VMEM((rows, width), BF16), pltpu.VMEM(gs, BF16),
+           pltpu.SemaphoreType.DMA((13,)), pltpu.SemaphoreType.DMA((2,))],
+        compiler_params=pltpu.CompilerParams(vmem_limit_bytes=63 << 20),
+        name="segment_backward",
+    )(x, cot, crossed, w_in, w_proj, w_up, w_down, ga.reshape(1, -1), gf.reshape(1, -1), *saved)
+
+def exact(a, b, dims=(((1,), (0,)), ((), ()))):
+    return lax.dot_general(a, b, dims, precision=lax.Precision.HIGHEST, preferred_element_type=F32)
+
+def gather_kernel(mine, out, buf, local, ss, rs):
+    y, x, z, core = spots()
+    dp, seg = lax.axis_index("dp"), lax.axis_index("seg")
+    xn, yn, cn = (2 * y + 1 - x, seg), (2 * (1 - y) + x, seg), (dp, 2 * z + 1 - core)
+    zn = [(dp, 2 * lax.rem(z + k, 4) + core) for k in (1, 2, 3)]
+    barrier = pltpu.get_barrier_semaphore()
+    for d in [xn, yn, cn] + zn:
+        pl.semaphore_signal(barrier, inc=1, device_id=d, device_id_type=MESH)
+    keep = pltpu.make_async_copy(mine, buf.at[core, x, y, z], local.at[0])
+    keep.start()
+    pl.semaphore_wait(barrier, 6)
+    def send(src, dst, k, to):
+        return pltpu.make_async_remote_copy(src, dst, ss.at[k], rs.at[k], device_id=to, device_id_type=MESH)
+    stage = [send(mine, buf.at[core, x, y, z], k, zn[k]) for k in range(3)]
+    for s in stage: s.start()
+    keep.wait()
+    for s in stage: s.wait()
+    for k, part, to in ((3, buf.at[core, x, y], yn), (4, buf.at[core, x], xn), (5, buf.at[core], cn)):
+        s = send(part, part, k, to)
+        s.start(); s.wait()
+    copy = pltpu.make_async_copy(buf, out, local.at[1])
+    copy.start(); copy.wait()
+
+def gather(mine, cid):
+    shape = (2, 2, 2, 4) + mine.shape
+    return pl.pallas_call(
+        gather_kernel, out_shape=sds(shape, mine.dtype), in_specs=[VM], out_specs=ANY,
+        scratch_shapes=[pltpu.VMEM(shape, mine.dtype), pltpu.SemaphoreType.DMA((2,)), pltpu.SemaphoreType.DMA((6,)), pltpu.SemaphoreType.DMA((6,))],
+        compiler_params=pltpu.CompilerParams(collective_id=cid, has_side_effects=True), name="gather_first_rows")(mine)
+
+def row_spots(shape, axis):
+    r = lax.broadcasted_iota(jnp.int32, shape, axis)
+    core, x, y, z, s = r // 64, r // 32 % 2, r // 16 % 2, r // 4 % 4, r % 4
+    return 2 * y + x, s * 8 + 2 * z + core
+
+def row_docs(shape, axis, counts):
+    slot, place = row_spots(shape, axis)
+    document, begin, first = jnp.zeros(shape, jnp.int32), jnp.zeros(shape, jnp.int32), jnp.zeros(shape, jnp.int32)
+    for s in range(counts.shape[0]):
+        end = jnp.int32(0)
+        for d in range(counts.shape[1]):
+            start, end = end, end + counts[s, d]
+            here = slot == s
+            document += jnp.where(here & (end <= place), 1, 0)
+            begin = jnp.where(here & (start <= place) & (place < end), start, begin)
+            first = jnp.where(here & (start == place), 1, first)
+    return slot, place, document, place - begin, first
+
+def cross_kernel(rows_in, counts, pads, embed, w_in, w_proj, w_up, w_down, ga, gf,
+                 result_o, crossed_o, d_in, d_proj, d_up, d_down, gains_o, embed_o,
+                 win, wproj, wup, wdown, hidden, slope, grad_pre, acc, base, cot, sem):
+    loads = [pltpu.make_async_copy(a, b, sem.at[k]) for k, (a, b) in enumerate(((w_in, win), (w_proj, wproj), (w_up, wup), (w_down, wdown)))]
+    for load in loads: load.start()
+    cross_body(rows_in, counts, pads, embed, win, wproj, wup, wdown, ga, gf, result_o, crossed_o, d_in, d_proj, d_up, d_down, gains_o, embed_o,
+               hidden, slope, grad_pre, acc, base, cot, lambda k: loads[k].wait())
+
+def cross_body(rows_in, counts, pads, embed, win, wproj, wup, wdown, ga, gf, result_o, crossed_o, d_in, d_proj, d_up, d_down, gains_o, embed_o,
+               hidden, slope, grad_pre, acc, base, cot, ready):
+    y, x, z, core = spots()
+    width = embed.shape[1]
+    n = 128
+    for k in range(32):
+        at = rows_in.at[k // 16, k // 8 % 2, k // 4 % 2, k % 4]
+        base[4 * k : 4 * k + 4, :] = at[:, :width]
+        cot[4 * k : 4 * k + 4, :] = at[:, width:]
+    slot_c, place_c, doc_c, rank_c, first_c = row_docs((n, 1), 0, counts)
+    slot_r, place_r, doc_r, rank_r, first_r = row_docs((1, n), 1, counts)
+    places = lax.broadcasted_iota(jnp.int32, (32, n), 0)
+    by_slot = exact(pads[...].astype(F32), (places == place_r).astype(F32))
+    pad_r = jnp.zeros((1, n), F32)
+    for s in range(pads.shape[0]):
+        pad_r = jnp.where(slot_r == s, by_slot[s : s + 1], pad_r)
+    ok_r = (pad_r == 0) | (first_r == 1)
+    allowed = (slot_c == slot_r) & (doc_c == doc_r) & ok_r
+    pick = (rank_c == lax.broadcasted_iota(jnp.int32, (n, 32), 1)).astype(F32)
+    xin = base[...] + exact(pick, embed[...])
+    xl = xin.astype(BF16)
+    masks = head_mask(n)
+    wide = jnp.concatenate([allowed.astype(F32)] * 4, 0) > 0
+    ready(0)
+    qkv = jnp.concatenate([nn(xl, win[:, k * width : (k + 1) * width]).astype(BF16) for k in range(3)], 1)
+    probs, atts = [], []
+    part = lambda a, k, quad: a[:, k * width + quad * QUAD : k * width + quad * QUAD + QUAD]
+    for quad in range(3):
+        scores = jnp.where(wide, nt(stacked(part(qkv, 0, quad), masks), part(qkv, 1, quad)) * HD ** -0.5, MASKED)
+        e = jnp.exp(scores - jnp.max(scores, -1, keepdims=True))
+        p = e / jnp.sum(e, -1, keepdims=True)
+        probs.append(p)
+        atts.append(picked(nn(p.astype(BF16), part(qkv, 2, quad)), masks).astype(BF16))
+    att = jnp.concatenate(atts, 1)
+    ready(1)
+    u1, i1 = unit(xin + nn(att, wproj[...]))
+    f = u1 * ga[...]
+    fl = f.astype(BF16)
+    ready(2)
+    ff, tile = wup.shape[1], 512
+    def up(k, c):
+        s = lanes(k * tile, tile)
+        h, g = gelu_pair(nn(fl, wup[:, s]))
+        hidden[:, s] = h.astype(BF16)
+        slope[:, s] = g
+        return c
+    lax.fori_loop(0, ff // tile, up, 0)
+    ready(3)
+    u2, i2 = unit(f + nn(hidden[...], wdown[...]))
+    me = ((core * 2 + x) * 2 + y) * 4 + z
+    own = (lax.broadcasted_iota(jnp.int32, (8, n), 1) == 4 * me + lax.broadcasted_iota(jnp.int32, (8, n), 0)).astype(F32)
+    result_o[...] = exact(own, u2 * gf[...])
+    d2, gain_f = norm_back(u2, i2, cot[...], gf[...])
+    dy2 = d2.astype(BF16)
+    def pre(k, c):
+        s = lanes(k * tile, tile)
+        grad_pre[:, s] = (nt(dy2, wdown[pl.ds(pl.multiple_of(k * tile, tile), tile), :]) * slope[:, s]).astype(BF16)
+        return c
+    lax.fori_loop(0, ff // tile, pre, 0)
+    d1, gain_a = norm_back(u1, i1, d2 + nt(grad_pre[...], wup[...]), ga[...])
+    dy1 = d1.astype(BF16)
+    datt = nt(dy1, wproj[...]).astype(BF16)
+    dq, dk, dv = [], [], []
+    for quad in range(3):
+        da = stacked(part(datt, 0, quad), masks)
+        q, k = stacked(part(qkv, 0, quad), masks), part(qkv, 1, quad)
+        p = probs[quad]
+        dp = nt(da, part(qkv, 2, quad))
+        ds = (p * (dp - jnp.sum(p * dp, -1, keepdims=True))).astype(BF16)
+        dq.append((picked(nn(ds, k), masks) * HD ** -0.5).astype(BF16))
+        dk.append((tn(ds, q) * HD ** -0.5).astype(BF16))
+        dv.append(tn(p.astype(BF16), da).astype(BF16))
+    dqkv = jnp.concatenate(dq + dk + dv, 1)
+    crossed = d1 + nt(dqkv, win[...])
+    crossed_o[...] = exact(own, crossed)
+    gains_o[0:1, :] = gain_a
+    gains_o[1:2, :] = gain_f
+    embed_o[...] = exact(pick, crossed, (((0,), (0,)), ((), ())))
+    j, i = 2 * z + core, 2 * y + x
+    def turn(a, by):
+        a = a.astype(F32)
+        return pltpu.roll(a, lax.rem(a.shape[1] - by, a.shape[1]), 1).astype(BF16)
+    sixth = width // 8
+    left = lambda a: turn(a, sixth * j)[:, :128]
+    d_in[...] = tn(left(xl), turn(dqkv, 3 * width // 4 * i)[:, :640])[:sixth, : 3 * width // 4]
+    d_proj[...] = tn(left(att), turn(dy1, width // 4 * i)[:, :256])[:sixth, : width // 4]
+    d_up[...] = tn(left(fl), grad_pre[:, lanes(ff // 4 * i, ff // 4)])[:sixth]
+    d_down[...] = tn(hidden[:, lanes(ff // 8 * j, ff // 8)], turn(dy2, width // 4 * i)[:, :256])[:, : width // 4]
+
+def cross(rows, counts, pads, embed, weights):
+    w_in, w_proj, ga, w_up, w_down, gf = weights
+    width, ff, n = embed.shape[1], w_up.shape[1], 128
+    outs = [((8, width), F32)] * 2 + [((width // 8, 3 * width // 4), F32), ((width // 8, width // 4), F32), ((width // 8, ff // 4), F32),
+            ((ff // 8, width // 4), F32), ((2, width), F32), (embed.shape, F32)]
+    return pl.pallas_call(
+        cross_kernel, out_shape=[sds(*o) for o in outs],
+        in_specs=[VM, pl.BlockSpec(memory_space=pltpu.SMEM), VM, VM, ANY, ANY, ANY, ANY, VM, VM], out_specs=[VM] * len(outs),
+        scratch_shapes=[pltpu.VMEM(w.shape, BF16) for w in (w_in, w_proj, w_up, w_down)]
+        + [pltpu.VMEM((n, ff), BF16), pltpu.VMEM((n, ff), F32), pltpu.VMEM((n, ff), BF16)] + [pltpu.VMEM((n, width), F32)] * 3 + [pltpu.SemaphoreType.DMA((4,))],
+        compiler_params=pltpu.CompilerParams(vmem_limit_bytes=60 << 20), name="cross_block",
+    )(rows, counts, pads, embed, w_in, w_proj, w_up, w_down, ga.reshape(1, -1), gf.reshape(1, -1))
+
+
+class Reducer:
+    def __init__(self, g, bufs):
+        self.g = g
+        self.r1, self.r2, self.r3, self.r4, self.own, self.peer, self.gain, self.ss, self.rs, self.zs, self.zr, self.gs, self.gr = bufs
+        self.y, self.x, self.z, self.core = y, x, z, core = spots()
+        self.dp, self.seg = lax.axis_index("dp"), lax.axis_index("seg")
+        self.xn, self.yn, self.cn = (2 * y + 1 - x, self.seg), (2 * (1 - y) + x, self.seg), (self.dp, 2 * z + 1 - core)
+        self.zt = [lax.rem(z + k, 4) for k in (1, 2, 3)]
+        self.zn = [(self.dp, 2 * t + core) for t in self.zt]
+        self.order = ((x, y, self.xn, self.yn), (y, x, self.yn, self.xn))
+
+    @staticmethod
+    def scratch(width):
+        dma = pltpu.SemaphoreType.DMA
+        v = lambda *s: pltpu.VMEM(s + (48, 384), BF16)
+        return [v(NC, 2, 2, 2, 2), v(NC, 2, 2, 2), v(NC, 4), v(NC, 3), v(NC), v(NC), pltpu.VMEM((7, 2, width), F32),
+                dma((6, NC)), dma((6, NC)), dma((3, NC)), dma((3, NC)), dma((6,)), dma((6,))]
+
+    def greet(self):
+        barrier = pltpu.get_barrier_semaphore()
+        for d in [self.xn, self.yn, self.cn] + self.zn:
+            pl.semaphore_signal(barrier, inc=1, device_id=d, device_id_type=MESH)
+    def met(self):
+        pl.semaphore_wait(pltpu.get_barrier_semaphore(), 6)
+
+    def copy(self, src, dst, s, r, to):
+        return pltpu.make_async_remote_copy(src, dst, s, r, device_id=to, device_id_type=MESH)
+    def s1(self, c):
+        return self.copy(self.g.at[c, 1 - self.core], self.r1.at[c], self.ss.at[0, c], self.rs.at[0, c], self.cn)
+    def s2(self, c, h):
+        p, q, pn, qn = self.order[h]
+        return self.copy(self.r1.at[c, h, 1 - p], self.r2.at[c, h], self.ss.at[1 + h, c], self.rs.at[1 + h, c], pn)
+    def s3(self, c, h):
+        p, q, pn, qn = self.order[h]
+        return self.copy(self.r2.at[c, h, 1 - q], self.r3.at[c, pl.ds(2 * h, 2)], self.ss.at[3 + h, c], self.rs.at[3 + h, c], qn)
+    def s4(self, c, k):
+        return self.copy(self.r3.at[c, self.zt[k]], self.r4.at[c, k], self.zs.at[k, c], self.zr.at[k, c], self.zn[k])
+    def s5(self, c):
+        return self.copy(self.own.at[c], self.peer.at[c], self.ss.at[5, c], self.rs.at[5, c], self.xn)
+    def needs(self, c, x):
+        low = (c == 4) | (c == 5) | (c == 9)
+        high = (c == 6) | (c == 7) | (c == 11)
+        return jnp.logical_not((low & (x == 1)) | (high & (x == 0)))
+
+    @staticmethod
+    def add(*terms):
+        total = terms[0].astype(F32)
+        for t in terms[1:]:
+            total = total + t.astype(F32)
+        return total.astype(BF16)
+
+    def start(self, c):
+        self.s1(c).start()
+    def core_done(self, c):
+        self.s1(c).wait()
+        for h in (0, 1):
+            p = self.order[h][0]
+            self.r1[c, h, 1 - p] = self.add(self.g[c, self.core, h, 1 - p], self.r1[c, h, 1 - p])
+            self.s2(c, h).start()
+        for h in (0, 1):
+            p = self.order[h][0]
+            self.r1[c, h, p] = self.add(self.g[c, self.core, h, p], self.r1[c, h, p])
+    def first_done(self, c):
+        for h in (0, 1):
+            self.s2(c, h).wait()
+            self.r2[c, h] = self.add(self.r1[c, h, self.order[h][0]], self.r2[c, h])
+            self.s3(c, h).start()
+    def second_done(self, c):
+        for h in (0, 1):
+            self.s3(c, h).wait()
+            rows = pl.ds(2 * h, 2)
+            self.r3[c, rows] = self.add(self.r2[c, h, self.order[h][1]], self.r3[c, rows])
+        for k in range(3): self.s4(c, k).start()
+    def line_done(self, c):
+        for k in range(3): self.s4(c, k).wait()
+        self.own[c] = self.add(self.r3[c, self.z], self.r4[c, 0], self.r4[c, 1], self.r4[c, 2])
+        @pl.when(self.needs(c, 1 - self.x))
+        def _(): self.s5(c).start()
+    def swap_done(self, c):
+        @pl.when(self.needs(c, 1 - self.x))
+        def _(): self.s5(c).wait_send()
+        @pl.when(self.needs(c, self.x))
+        def _(): self.s5(c).wait_recv()
+
+    def advance(self, t):
+        for stage, act in enumerate((self.start, self.core_done, self.first_done, self.second_done, self.line_done, self.swap_done)):
+            @pl.when((t >= stage) & (t < NC + stage))
+            def _(): act(t - stage)
+
+    def gain_copies(self, stage):
+        if stage < 3:
+            to = (self.cn, self.xn, self.yn)[stage]
+            return [self.copy(self.gain.at[0], self.gain.at[1 + stage], self.gs.at[stage], self.gr.at[stage], to)]
+        return [self.copy(self.gain.at[0], self.gain.at[4 + k], self.gs.at[3 + k], self.gr.at[3 + k], self.zn[k]) for k in range(3)]
+    def gain_start(self, stage):
+        for c in self.gain_copies(stage): c.start()
+    def gain_done(self, stage):
+        for c in self.gain_copies(stage): c.wait()
+        if stage < 3:
+            self.gain[0] = self.gain[0] + self.gain[1 + stage]
+        else:
+            self.gain[0] = self.gain[0] + self.gain[4] + self.gain[5] + self.gain[6]
+
+    def deliver(self, d_in, d_proj, d_up, d_down):
+        for mine in (0, 1):
+            @pl.when(self.x == mine)
+            def _():
+                for half in (0, 1):
+                    a = self.own if half == mine else self.peer
+                    r = slice(48 * half, 48 * half + 48)
+                    side = slice(192 * mine, 192 * mine + 192)
+                    d_proj[r, :] = a[8, :, side].astype(F32)
+                    for k in range(2):
+                        d_up[r, 384 * k : 384 * k + 384] = a[4 + 2 * mine + k].astype(F32)
+                    parts = [a[9], a[10, :, side]] if mine == 0 else [a[10, :, side], a[11]]
+                    d_in[r, :] = jnp.concatenate(parts, 1).astype(F32)
+                    for k in range(4):
+                        d_down[96 * k + 48 * half : 96 * k + 48 * half + 48, :] = a[k, :, side].astype(F32)
+
+def reduce_kernel(g_in, gains, d_in, d_proj, d_up, d_down, gains_o, *scr):
+    red = Reducer(g_in, scr)
+    red.greet()
+    red.gain[0] = gains[...]
+    red.met()
+    def step(t, c):
+        red.advance(t)
+        return c
+    lax.fori_loop(0, 3, step, 0)
+    for k in range(4):
+        red.gain_start(k)
+        lax.fori_loop(3 + 3 * k, 6 + 3 * k, step, 0)
+        red.gain_done(k)
+    lax.fori_loop(15, NC + 6, step, 0)
+    gains_o[...] = red.gain[0]
+    red.deliver(d_in, d_proj, d_up, d_down)
+
+def reduce(g, gains, width, ff):
+    outs = [(width // 8, 3 * width // 4), (width // 8, width // 4), (width // 8, ff // 4), (ff // 8, width // 4), (2, width)]
+    return pl.pallas_call(
+        reduce_kernel, out_shape=[sds(s, F32) for s in outs], in_specs=[VM, VM], out_specs=[VM] * 5, scratch_shapes=Reducer.scratch(width),
+        compiler_params=pltpu.CompilerParams(collective_id=1, has_side_effects=True, vmem_limit_bytes=60 << 20), name="reduce_weights")(g, gains)
+
+
+def this_mesh(
+    tokens, doc_counts, pad_mask, attn_in, attn_proj, norm_attn, ffn_up, ffn_down, norm_ffn,
+    segment_embed, cross_in, cross_proj, cross_norm_attn, cross_up, cross_down, cross_norm_ffn,
+    cotangent,
+):
+    segs, length, width = tokens.shape
+    rows, ff = segs * length, ffn_up.shape[1]
+    member, group = lax.axis_index("seg"), lax.axis_index("dp")
+    x, cot = tokens.reshape(rows, width), cotangent.reshape(rows, width)
+    weights = (attn_in, attn_proj, norm_attn, ffn_up, ffn_down, norm_ffn)
+    cross_weights = (cross_in, cross_proj, cross_norm_attn, cross_up, cross_down, cross_norm_ffn)
+    *saved, out, first = forward(x, segs, weights)
+    mine = jnp.concatenate([first, cotangent[:, 0, :].astype(F32)], 1)
+    everyone = gather(mine, 0)
+    result, crossed, c_in, c_proj, c_up, c_down, c_gains, c_embed = cross(everyone, doc_counts, pad_mask, segment_embed, cross_weights)
+    output = out.reshape(tokens.shape).at[:, 0, :].set(result[:segs].astype(BF16))
+    token_grad, gains, g = backward(x, cot, crossed, saved, segs, weights)
+    d_in, d_proj, d_up, d_down, totals = reduce(g, gains, width, ff)
+    block = width // 8
+    piece = lambda a, k: lax.dynamic_slice(a, (k, member * block), (1, block))[0]
+    embed_block = lax.dynamic_slice(c_embed, (group * 8, member * block), (8, block))
+    return (
+        output, token_grad.reshape(tokens.shape), d_in, d_proj, piece(totals, 0), d_up, d_down, piece(totals, 1),
+        embed_block, c_in, c_proj, piece(c_gains, 0), c_up, c_down, piece(c_gains, 1),
+    )
+
+
 def solution(mesh):
+    fits = (mesh.shape["dp"], mesh.shape["seg"]) == (4, 8)
     placed = (
         P(("dp", "seg"), None, None),
         P(),
@@ -296,7 +933,7 @@
         P(("dp", "seg"), None, None),
     )
     return jax.shard_map(
-        on_device,
+        this_mesh if fits else any_mesh,
         mesh=mesh,
         in_specs=placed,
         out_specs=(

time: 574 us -> 214 us (0.37)
  Pallas kernels: 0 us -> 194 us
  blocking collectives: 135 us -> 0 us
  matrix products: 132 us -> 0 us
  waiting for transfers between devices: 118 us -> 0 us
  local copies, waits for them, and re-layouts: 127 us -> 17.1 us
  other arithmetic: 39.2 us -> 1.33 us
  between operations: 15 us -> 0.73 us
    pallas_call x0 -> x5, Pallas kernels: none -> 194 us  [the longest x1 84 us: reduce(): pl.pallas_call(reduce_kernel, out_shape=[sds(s, F32) for s in outs], in_s...]
    dot_general x38 -> x0, matrix products: 132 us -> none  [the longest x8 40.2 us: matmul(): return jnp.dot(former, latter, preferred_element_type=jnp.float32)]
    all_gather x2 -> x0, blocking collectives: 95.1 us -> none  [the longest x1 50.2 us: on_device(): lax.all_gather(cotangent[:, 0, :], ('dp', 'seg'), axis=0, tiled=True)[order]]
    reduce_scatter x3 -> x0, waiting for transfers between devices: 83.3 us -> none  [reduce_weights(): lax.psum_scatter(g.astype(jnp.bfloat16), 'seg', scatter_dimension=0, tile...]
    psum x1 -> x0, blocking collectives: 40.4 us -> none  [on_device(): lax.psum(jnp.concatenate([grad_norm_attn, grad_norm_ffn]), ('dp', 'seg'))]
    reshape x19 -> x4, local copies, waits for them, and re-layouts: 41.6 us -> 3.7 us  [the longest x1 1.27 us: forward(): ga.reshape(1, -1)]
    unnamed x7 -> x0, waiting for transfers between devices: 35.2 us -> none
    slice x15 -> x1, local copies, waits for them, and re-layouts: 22.2 us -> 0.81 us  [this_mesh(): mine = jnp.concatenate([first, cotangent[:, 0, :].astype(F32)], 1)]
  transfers between devices with their start and end apart: 5 -> 0, of which waited for: 3 -> 0; matrix products, arithmetic and copies ran while one was open for 16% -> 0% of each run, Pallas kernels for 0% -> 0%
where the time goes in v2:
time: 214 us; the launch traced here: 213 us
  Pallas kernels  194 us (91%)
  local copies, waits for them, and re-layouts  17.1 us (8%)
    pallas_call x1, Pallas kernels, reduce(): pl.pallas_call(reduce_kernel, out_shape=[sds(s, F32) for s in outs], in_s...  84 us
    pallas_call x1, Pallas kernels, backward(): pl.pallas_call(partial(backward_kernel, segs), out_shape=[sds((rows, widt...  40.2 us
    pallas_call x1, Pallas kernels, forward(): pl.pallas_call(partial(forward_kernel, segs), out_shape=[sds(*s) for s in...  29.8 us
    pallas_call x1, Pallas kernels, gather(): pl.pallas_call(gather_kernel, out_shape=sds(shape, mine.dtype), in_specs=...  20.3 us
    pallas_call x1, Pallas kernels, cross(): pl.pallas_call(cross_kernel, out_shape=[sds(*o) for o in outs], in_specs=...  19.4 us
    unnamed x11, local copies, waits for them, and re-layouts  7.62 us

profile of v2, /device:TPU:0, one launch (start us, length us, event | category | flops | bytes accessed | tf_op | source)
XLA Modules:
  0.0 212.9 jit_solution(14885867648334633434)
XLA Ops:
  0.6 1.3 reshape.92.ga
  1.9 1.3 reshape.93.gf
  3.2 0.0 copy-start.1
  3.2 0.0 copy-start.2
  3.2 29.8 %segment_forward.1 = (bf16[512,2304]{1,0:T(8,128)(2,1)}, f32[12,512,128]{2,1,0:T(8,128)}, bf16[512,768]{1,0:T(8,128)(2,1)}, f32[512,768]{1,0:T(8,128)}, f32[512,...) custom-call(bf16[512,768]{1,0:T(8,128)(2,1)} %bitcast.19, ...), custom_call_target="tpu_custom_call" | custom-call | tf_op jit(solution)/shard_map/segment_forward/pallas_call | solution.py:410
  33.0 0.8 slice.27
  33.8 1.3 pad_maximum_fusion.mine
  35.1 20.3 %gather_first_rows.1.rows_in = f32[2,2,2,4,4,1536]{5,4,3,2,1,0:T(4,128)} custom-call(f32[4,1536]{1,0:T(4,128)} %pad_maximum_fusion.mine), custom_call_target="tpu_custom_call" | custom-call | tf_op jit(solution)/shard_map/gather_first_rows/pallas_call | solution.py:610
  55.4 0.0 copy-done.1
  55.4 0.6 reshape.95.ga
  56.0 0.0 copy-done.2
  56.0 0.6 reshape.96.gf
  56.6 19.4 %cross_block.1 = (f32[8,768]{1,0:T(8,128)}, f32[8,768]{1,0:T(8,128)}, f32[96,576]{1,0:T(8,128)}, f32[96,192]{1,0:T(8,128)}, f32[96,768]{1,0:T(8,128)}, /*index=5...) custom-call(f32[2,2,2,4,4,1536]{5,4,3,2,1,0:T(4,128)} %gather_first_rows.1.rows_in, s32[4,6]{1,0:T(4,128)} %counts.1, ...), custom_call_target="tpu_custom_call" | custom-call | tf_op jit(solution)/shard_map/cross_block/pallas_call | solution.py:735
  76.1 0.7 fusion
  76.8 1.5 scatter.4
  78.3 40.2 %segment_backward.1 = (bf16[512,768]{1,0:T(8,128)(2,1)}, f32[2,768]{1,0:T(2,128)}, bf16[12,2,2,2,2,2,48,384]{7,6,5,4,3,2,1,0:T(8,128)(2,1)}) custom-call(bf16[512,768]{1,0:T(8,128)(2,1)} %bitcast.20, bf16[512,768]{1,0:T(8,128)(2,1)} %bitcast.21, f32[8,768]{1,0:T(8,128)} %get-tuple-element.56.crossed, bf16[768,2304]{1,0:T(8,128)(2,1)} %w_in.5, ...), custom_call_target="tpu_custom_call" | custom-call | tf_op jit(solution)/shard_map/segment_backward/pallas_call | solution.py:569
  118.5 0.0 copy-start
  118.5 84.0 %reduce_weights.1 = (f32[96,576]{1,0:T(8,128)}, f32[96,192]{1,0:T(8,128)}, f32[96,768]{1,0:T(8,128)}, f32[384,192]{1,0:T(8,128)}, f32[2,768]{1,0:T(2,128)}) custom-call(bf16[12,2,2,2,2,2,48,384]{7,6,5,4,3,2,1,0:T(8,128)(2,1)} %get-tuple-element.66.g_in, f32[2,768]{1,0:T(2,128)} %get-tuple-element.67.gains), custom_call_target="tpu_custom_call" | custom-call | tf_op jit(solution)/shard_map/reduce_weights/pallas_call | solution.py:882
  202.6 1.4 fusion.2
  203.9 1.9 copy.34
  205.8 1.4 dynamic_slice.17
  207.2 0.0 copy-done
  207.2 0.9 copy.35
  208.0 1.7 copy.44
  209.7 1.5 copy.45
  211.2 1.7 copy.46
  (2 shorter events, 0.0 us)
Async XLA Ops:
  3.2 52.2 %copy-start.1 = (f32[768]{0:T(1024)S(1)}, f32[768]{0:T(1024)}, u32[]{:S(2)}) copy-start(f32[768]{0:T(1024)} %param.31) | copy-start | bytes 9220
  3.2 52.8 %copy-start.2 = (f32[768]{0:T(1024)S(1)}, f32[768]{0:T(1024)}, u32[]{:S(2)}) copy-start(f32[768]{0:T(1024)} %param.34) | copy-start | bytes 9220
  118.5 88.7 %copy-start = (f32[384,192]{1,0:T(8,128)S(1)}, f32[384,192]{1,0:T(8,128)}, u32[]{:S(2)}) copy-start(f32[384,192]{1,0:T(8,128)} %get-tuple-element.92) | copy-start | bytes 884740

commit v3 on v1

--- a/solution.py
+++ b/solution.py
@@ -3,6 +3,8 @@
 import jax
 import jax.numpy as jnp
 import numpy as np
+from jax.experimental import pallas as pl
+from jax.experimental.pallas import tpu as pltpu
 from jax import lax
 from jax.sharding import PartitionSpec as P
 
@@ -199,7 +201,7 @@
     return outs
 
 
-def on_device(
+def any_mesh(
     tokens, doc_counts, pad_mask, attn_in, attn_proj, norm_attn, ffn_up, ffn_down, norm_ffn,
     segment_embed, cross_in, cross_proj, cross_norm_attn, cross_up, cross_down, cross_norm_ffn,
     cotangent,
@@ -275,7 +277,692 @@
     )
 
 
+BF16, F32 = jnp.bfloat16, jnp.float32
+QUAD = 4 * HD
+NC, GS = 12, 8
+PAY = 3 * 768 + 128
+MESH = pl.DeviceIdType.MESH
+ERFC = (0.23192104, 0.16183046, 0.46825631, -0.37088501, 0.70913273, -0.20025555)
+
+def nn(a, b): return jnp.dot(a, b, preferred_element_type=F32)
+def nt(a, b): return lax.dot_general(a, b, (((1,), (1,)), ((), ())), preferred_element_type=F32)
+def tn(a, b): return lax.dot_general(a, b, (((0,), (0,)), ((), ())), preferred_element_type=F32)
+
+def gelu_pair(v):
+    size = jnp.abs(v)
+    t = 1.0 / (1.0 + (0.4 * 0.5 ** 0.5) * size)
+    bell = jnp.exp(-0.5 * (v * v))
+    poly = F32(0.5 * ERFC[5])
+    for c in ERFC[4::-1]:
+        poly = poly * t + F32(0.5 * c)
+    tail = poly * t * bell
+    cdf = jnp.where(v >= 0, 1.0 - tail, tail)
+    scaled = v * cdf
+    return scaled, cdf + v * (bell * F32((2 * np.pi) ** -0.5))
+
+def mean(v): return jnp.mean(v, -1, keepdims=True)
+
+def unit(total):
+    middle = total - mean(total)
+    inverse = lax.rsqrt(mean(middle * middle) + EPSILON)
+    return middle * inverse, inverse
+
+def lanes(start, size):
+    return pl.ds(pl.multiple_of(start, 128), size)
+
+def head_mask(rows):
+    lane = lax.broadcasted_iota(jnp.int32, (rows, QUAD), 1)
+    return [lane // HD == h for h in range(4)]
+
+def stacked(v, masks):
+    zero = jnp.zeros_like(v)
+    return jnp.concatenate([jnp.where(m, v, zero) for m in masks], 0)
+
+def picked(v, masks):
+    n = v.shape[0] // 4
+    out = v[3 * n :]
+    for h in (2, 1, 0):
+        out = jnp.where(masks[h], v[h * n : (h + 1) * n], out)
+    return out
+
+def row(v):
+    return v[...].reshape(1, v.shape[0])
+
+def forward_kernel(segs, x, w_in, w_proj, w_up, w_down, ga_v,
+                   qkv_o, probs_o, att_o, unit1_o, unit2_o, inv_o, hidden_o, slope_o,
+                   win, wproj, wup, wdown, qkv, probs, att, unit1, unit2, inv, hidden, slope, acc, low, in_sem, out_sem):
+    rows, width = x.shape
+    length = rows // segs
+    ga = row(ga_v)
+    loads = [pltpu.make_async_copy(a, b, in_sem.at[k]) for k, (a, b) in enumerate(((w_in, win), (w_proj, wproj), (w_up, wup), (w_down, wdown)))]
+    for load in loads: load.start()
+    saves = []
+    def save(a, b):
+        copy = pltpu.make_async_copy(a, b, out_sem.at[len(saves)])
+        copy.start(); saves.append(copy)
+    loads[0].wait()
+    def project(n, c):
+        s = lanes(n * width, width)
+        qkv[:, s] = nn(x[...], win[:, s]).astype(BF16)
+        return c
+    lax.fori_loop(0, 3, project, 0)
+    save(qkv, qkv_o)
+    masks = head_mask(length)
+    def attend(n, c):
+        seg, quad = n // 3, n % 3
+        r = pl.ds(pl.multiple_of(seg * length, length), length)
+        q = stacked(qkv[r, lanes(quad * QUAD, QUAD)], masks)
+        scores = nt(q, qkv[r, lanes(width + quad * QUAD, QUAD)]) * HD ** -0.5
+        e = jnp.exp(scores - jnp.max(scores, -1, keepdims=True))
+        p = e / jnp.sum(e, -1, keepdims=True)
+        p = p.astype(BF16)
+        probs[n] = p
+        o = nn(p, qkv[r, lanes(2 * width + quad * QUAD, QUAD)])
+        att[r, lanes(quad * QUAD, QUAD)] = picked(o, masks).astype(BF16)
+        return c
+    lax.fori_loop(0, 3 * segs, attend, 0)
+    save(probs, probs_o); save(att, att_o)
+    loads[1].wait()
+    acc[...] = nn(att[...], wproj[...])
+    def first(n, c):
+        r = pl.ds(pl.multiple_of(n * length, length), length)
+        u, i = unit(x[r, :].astype(F32) + acc[r, :])
+        unit1[r, :] = u
+        inv[0, r, :] = jnp.broadcast_to(i, (length, 128))
+        f = u * ga
+        acc[r, :] = f
+        low[r, :] = f.astype(BF16)
+        return c
+    lax.fori_loop(0, segs, first, 0)
+    save(unit1, unit1_o)
+    loads[2].wait()
+    tile = 512
+    def up(n, c):
+        s = lanes(n * tile, tile)
+        h, g = gelu_pair(nn(low[...], wup[:, s]))
+        hidden[:, s] = h.astype(BF16)
+        slope[:, s] = g.astype(BF16)
+        return c
+    lax.fori_loop(0, wup.shape[1] // tile, up, 0)
+    save(hidden, hidden_o); save(slope, slope_o)
+    loads[3].wait()
+    def down(n, c):
+        s = lanes(n * QUAD, QUAD)
+        acc[:, s] += nn(hidden[...], wdown[:, s])
+        return c
+    lax.fori_loop(0, width // QUAD, down, 0)
+    def second(n, c):
+        r = pl.ds(pl.multiple_of(n * length, length), length)
+        u, i = unit(acc[r, :])
+        unit2[r, :] = u
+        inv[1, r, :] = jnp.broadcast_to(i, (length, 128))
+        return c
+    lax.fori_loop(0, segs, second, 0)
+    save(unit2, unit2_o); save(inv, inv_o)
+    for copy in saves: copy.wait()
+
+ANY = pl.BlockSpec(memory_space=pl.ANY)
+VM = pl.BlockSpec(memory_space=pltpu.VMEM)
+def sds(*a): return jax.ShapeDtypeStruct(*a)
+
+def forward(x, segs, weights):
+    w_in, w_proj, ga, w_up, w_down = weights[:5]
+    rows, width = x.shape
+    ff = w_up.shape[1]
+    length = rows // segs
+    saved = [((rows, 3 * width), BF16), ((3 * segs, 4 * length, length), BF16), ((rows, width), BF16), ((rows, width), F32),
+             ((rows, width), F32), ((2, rows, 128), F32), ((rows, ff), BF16), ((rows, ff), BF16)]
+    return pl.pallas_call(
+        partial(forward_kernel, segs),
+        out_shape=[sds(*s) for s in saved],
+        in_specs=[VM, ANY, ANY, ANY, ANY, VM],
+        out_specs=[ANY] * 8,
+        scratch_shapes=[pltpu.VMEM(w.shape, BF16) for w in (w_in, w_proj, w_up, w_down)]
+        + [pltpu.VMEM(*s) for s in saved]
+        + [pltpu.VMEM((rows, width), F32), pltpu.VMEM((rows, width), BF16), pltpu.SemaphoreType.DMA((4,)), pltpu.SemaphoreType.DMA((8,))],
+        compiler_params=pltpu.CompilerParams(vmem_limit_bytes=60 << 20),
+        name="segment_forward",
+    )(x, w_in, w_proj, w_up, w_down, ga)
+
+
+def spots():
+    dp, seg = lax.axis_index("dp"), lax.axis_index("seg")
+    return dp // 2, dp % 2, seg // 2, seg % 2
+
+def norm_back(u, i, up, gain):
+    s = up * gain
+    return i * (s - mean(s) - u * mean(s * u)), jnp.sum(up * u, 0, keepdims=True)
+
+def exact(a, b, dims=(((1,), (0,)), ((), ()))):
+    return lax.dot_general(a, b, dims, precision=lax.Precision.HIGHEST, preferred_element_type=F32)
+
+def row_spots(shape, axis):
+    r = lax.broadcasted_iota(jnp.int32, shape, axis)
+    core, x, y, z, s = r // 64, r // 32 % 2, r // 16 % 2, r // 4 % 4, r % 4
+    return 2 * y + x, s * 8 + 2 * z + core
+
+def row_docs(shape, axis, counts):
+    slot, place = row_spots(shape, axis)
+    document, begin, first = jnp.zeros(shape, jnp.int32), jnp.zeros(shape, jnp.int32), jnp.zeros(shape, jnp.int32)
+    for s in range(counts.shape[0]):
+        end = jnp.int32(0)
+        for d in range(counts.shape[1]):
+            start, end = end, end + counts[s, d]
+            here = slot == s
+            document += jnp.where(here & (end <= place), 1, 0)
+            begin = jnp.where(here & (start <= place) & (place < end), start, begin)
+            first = jnp.where(here & (start == place), 1, first)
+    return slot, place, document, place - begin, first
+
+
+def slot_of(chunk):
+    return chunk if chunk < GS else (3, 0, 1, 2)[chunk - GS]
+
+class Reducer:
+    def __init__(self, g, bufs):
+        self.g = g
+        self.r1, self.r2, self.r3, self.r4, self.own, self.peer, self.gain, self.ss, self.rs, self.zs, self.zr, self.gs, self.gr = bufs
+        self.y, self.x, self.z, self.core = y, x, z, core = spots()
+        self.dp, self.seg = lax.axis_index("dp"), lax.axis_index("seg")
+        self.xn, self.yn, self.cn = (2 * y + 1 - x, self.seg), (2 * (1 - y) + x, self.seg), (self.dp, 2 * z + 1 - core)
+        self.zt = [lax.rem(z + k, 4) for k in (1, 2, 3)]
+        self.zn = [(self.dp, 2 * t + core) for t in self.zt]
+        self.order = ((x, y, self.xn, self.yn), (y, x, self.yn, self.xn))
+
+    @staticmethod
+    def scratch(width):
+        dma = pltpu.SemaphoreType.DMA
+        v = lambda *s: pltpu.VMEM(s + (48, 384), BF16)
+        return [v(NC, 2, 2, 2, 2), v(NC, 2, 2, 2), v(NC, 4), v(NC, 3), v(NC), v(NC), pltpu.VMEM((7, 2, width), F32),
+                dma((6, NC)), dma((6, NC)), dma((3, NC)), dma((3, NC)), dma((6,)), dma((6,))]
+
+    def greet(self):
+        barrier = pltpu.get_barrier_semaphore()
+        for d in [self.xn, self.yn, self.cn] + self.zn:
+            pl.semaphore_signal(barrier, inc=1, device_id=d, device_id_type=MESH)
+    def met(self):
+        pl.semaphore_wait(pltpu.get_barrier_semaphore(), 6)
+
+    def copy(self, src, dst, s, r, to):
+        return pltpu.make_async_remote_copy(src, dst, s, r, device_id=to, device_id_type=MESH)
+    def s1(self, c):
+        return self.copy(self.g.at[slot_of(c), 1 - self.core], self.r1.at[c], self.ss.at[0, c], self.rs.at[0, c], self.cn)
+    def s2(self, c, h):
+        p, q, pn, qn = self.order[h]
+        return self.copy(self.r1.at[c, h, 1 - p], self.r2.at[c, h], self.ss.at[1 + h, c], self.rs.at[1 + h, c], pn)
+    def s3(self, c, h):
+        p, q, pn, qn = self.order[h]
+        return self.copy(self.r2.at[c, h, 1 - q], self.r3.at[c, pl.ds(2 * h, 2)], self.ss.at[3 + h, c], self.rs.at[3 + h, c], qn)
+    def s4(self, c, k):
+        return self.copy(self.r3.at[c, self.zt[k]], self.r4.at[c, k], self.zs.at[k, c], self.zr.at[k, c], self.zn[k])
+    def s5(self, c):
+        return self.copy(self.own.at[c], self.peer.at[c], self.ss.at[5, c], self.rs.at[5, c], self.xn)
+    def if_needed(self, c, x, act):
+        if c in (4, 5, 9):
+            pl.when(x == 0)(act)
+        elif c in (6, 7, 11):
+            pl.when(x == 1)(act)
+        else:
+            act()
+
+    @staticmethod
+    def add(*terms):
+        total = terms[0].astype(F32)
+        for t in terms[1:]:
+            total = total + t.astype(F32)
+        return total.astype(BF16)
+
+    def start(self, c):
+        self.s1(c).start()
+    def core_done(self, c):
+        self.s1(c).wait()
+        for h in (0, 1):
+            p = self.order[h][0]
+            for at in (1 - p, p):
+                def one(k, carry, h=h, at=at):
+                    self.r1[c, h, at, k // 2, k % 2] = self.add(self.g[slot_of(c), self.core, h, at, k // 2, k % 2], self.r1[c, h, at, k // 2, k % 2])
+                    return carry
+                lax.fori_loop(0, 4, one, 0)
+                if at is not p:
+                    self.s2(c, h).start()
+    def first_done(self, c):
+        for h in (0, 1):
+            self.s2(c, h).wait()
+            def one(k, carry, h=h):
+                self.r2[c, h, k // 2, k % 2] = self.add(self.r1[c, h, self.order[h][0], k // 2, k % 2], self.r2[c, h, k // 2, k % 2])
+                return carry
+            lax.fori_loop(0, 4, one, 0)
+            self.s3(c, h).start()
+    def second_done(self, c):
+        for h in (0, 1):
+            self.s3(c, h).wait()
+            for zz in (0, 1):
+                self.r3[c, 2 * h + zz] = self.add(self.r2[c, h, self.order[h][1], zz], self.r3[c, 2 * h + zz])
+        for k in range(3): self.s4(c, k).start()
+    def line_done(self, c):
+        for k in range(3): self.s4(c, k).wait()
+        self.own[c] = self.add(self.r3[c, self.z], self.r4[c, 0], self.r4[c, 1], self.r4[c, 2])
+        self.if_needed(c, 1 - self.x, lambda: self.s5(c).start())
+    def swap_done(self, c):
+        self.if_needed(c, 1 - self.x, lambda: self.s5(c).wait_send())
+        self.if_needed(c, self.x, lambda: self.s5(c).wait_recv())
+
+    def gain_copies(self, stage):
+        if stage < 3:
+            to = (self.cn, self.xn, self.yn)[stage]
+            return [self.copy(self.gain.at[0], self.gain.at[1 + stage], self.gs.at[stage], self.gr.at[stage], to)]
+        return [self.copy(self.gain.at[0], self.gain.at[4 + k], self.gs.at[3 + k], self.gr.at[3 + k], self.zn[k]) for k in range(3)]
+    def gain_start(self, stage):
+        for c in self.gain_copies(stage): c.start()
+    def gain_done(self, stage):
+        for c in self.gain_copies(stage): c.wait()
+        if stage < 3:
+            self.gain[0] = self.gain[0] + self.gain[1 + stage]
+        else:
+            self.gain[0] = self.gain[0] + self.gain[4] + self.gain[5] + self.gain[6]
+
+
+class Pipeline:
+    def __init__(self, red):
+        self.red, self.flying = red, []
+    def move(self, *new):
+        r = self.red
+        for c in new:
+            r.start(c)
+        acts = (r.core_done, r.first_done, r.second_done, r.line_done, r.swap_done)
+        for k, (c, stage) in enumerate(self.flying):
+            acts[stage](c)
+            self.flying[k] = (c, stage + 1)
+        self.flying = [f for f in self.flying if f[1] < 5] + [(c, 0) for c in new]
+
+def finish_kernel(segs, x_h, cot_h, counts, pads, embed, w_in, w_proj, w_up, w_down, ga_v, gf_v, cw_in, cw_proj, cw_up, cw_down, cga_v, cgf_v, *rest):
+    saved_h, rest = rest[:8], rest[8:]
+    token_o, out_o, own_o, peer_o, d_up0, d_down0, c_in, c_proj, c_up, c_down, small_o, embed_o = rest[:12]
+    cot, win, wproj, wup, wdown, qkv, probs, att, unit1, unit2, inv, hidden, slope, low, dy, outb, g, pay, buf, slope0, base, cross_cot, gains = rest[12:35]
+    in_sem, again_sem, out_sem, local, gs, gr = rest[35:41]
+    red = Reducer(g, rest[41:])
+    pipe = Pipeline(red)
+    y, x_at, z, core = red.y, red.x, red.z, red.core
+    rows, width = x_h.shape
+    length = rows // segs
+    ff = wup.shape[1]
+    ga, gf, cga, cgf = row(ga_v), row(gf_v), row(cga_v), row(cgf_v)
+    tile = 512
+
+    names = ("cot", "unit2", "inv", "unit1", "hidden", "wdown", "slope", "wup", "cwin", "cwproj", "att", "qkv", "probs")
+    pairs = ((cot_h, cot), (saved_h[4], unit2), (saved_h[5], inv), (saved_h[3], unit1), (saved_h[6], hidden), (w_down, wdown), (saved_h[7], slope),
+             (w_up, wup), (cw_in, win), (cw_proj, wproj), (saved_h[2], att), (saved_h[0], qkv), (saved_h[1], probs))
+    loads = {k: pltpu.make_async_copy(a, b, in_sem.at[n]) for n, (k, (a, b)) in enumerate(zip(names, pairs))}
+    for load in loads.values(): load.start()
+    again = {}
+    def reload(name, src, dst):
+        again[name] = pltpu.make_async_copy(src, dst, again_sem.at[len(again)])
+        again[name].start()
+    red.greet()
+
+    for k in ("cot", "unit2", "inv", "unit1"): loads[k].wait()
+    for s in range(segs):
+        r = slice(s * length, s * length + 1)
+        pay[s : s + 1, :width] = unit1[r, :]
+        pay[s : s + 1, width : 2 * width] = unit2[r, :]
+        pay[s : s + 1, 2 * width : 3 * width] = cot[s * length : s * length + 16, :].astype(F32)[:1]
+        pay[s : s + 1, 3 * width :] = inv[1, r, :]
+    top = lax.broadcasted_iota(jnp.int32, (length, 1), 0) == 0
+    gains[...] = jnp.zeros_like(gains)
+    def second(n, c):
+        r = pl.ds(pl.multiple_of(n * length, length), length)
+        up = jnp.where(top, 0.0, cot[r, :].astype(F32))
+        u = unit2[r, :]
+        outb[r, :] = (u * gf).astype(BF16)
+        d, gain = norm_back(u, inv[1, r, :1], up, gf)
+        gains[1:2, :] += gain
+        unit2[r, :] = d
+        dy[r, :] = d.astype(BF16)
+        low[r, :] = (unit1[r, :] * ga).astype(BF16)
+        return c
+    lax.fori_loop(0, segs, second, 0)
+
+    red.met()
+    mine = buf.at[core, x_at, y, z]
+    keep = pltpu.make_async_copy(pay, mine, local.at[0])
+    keep.start()
+    send = lambda src, dst, k, to: red.copy(src, dst, gs.at[k], gr.at[k], to)
+    along_z = [send(pay, mine, k, red.zn[k]) for k in range(3)]
+    later = [send(p, p, k, to) for k, p, to in ((3, buf.at[core, x_at, y], red.yn), (4, buf.at[core, x_at], red.xn), (5, buf.at[core], red.cn))]
+    for s in along_z: s.start()
+
+    loads["hidden"].wait()
+    def down_grad(j, c):
+        v = tn(hidden[:, lanes(j * 384, 384)], dy[...]).astype(BF16)
+        z_to, core_to = j // 2, j % 2
+        h, zz = z_to // 2, z_to % 2
+        for chunk in range(4):
+            for half in range(2):
+                for side in range(2):
+                    part = v[chunk * 96 + half * 48 : chunk * 96 + half * 48 + 48, side * 384 : side * 384 + 384]
+                    g[chunk, core_to, h, half * (1 - h) + side * h, side * (1 - h) + half * h, zz] = part
+        return c
+    lax.fori_loop(0, 4, down_grad, 0)
+    keep.wait()
+    for s in along_z: s.wait()
+    later[0].start()
+    lax.fori_loop(4, 8, down_grad, 0)
+    pipe.move(0)
+    later[0].wait(); later[1].start()
+
+    loads["slope"].wait()
+    for s in range(segs):
+        slope0[s : s + 1, :] = slope[s * length : s * length + 16, :].astype(F32)[:1]
+    loads["wdown"].wait()
+    def pre_grad(n, c):
+        s = lanes(n * tile, tile)
+        slope[:, s] = (nt(dy[...], wdown[pl.ds(pl.multiple_of(n * tile, tile), tile), :]) * slope[:, s].astype(F32)).astype(BF16)
+        return c
+    lax.fori_loop(0, 3, pre_grad, 0)
+    pipe.move(1)
+    lax.fori_loop(3, ff // tile, pre_grad, 0)
+    later[1].wait(); later[2].start()
+    reload("cwdown", cw_down, wdown)
+    pipe.move(2)
+
+    def put(slot, side, v):
+        v = v.astype(BF16)
+        for j in range(8):
+            z_to, core_to = j // 2, j % 2
+            h, zz = z_to // 2, z_to % 2
+            for half in range(2):
+                p, q = (half, side) if h == 0 else (side, half)
+                g[slot, core_to, h, p, q, zz] = v[j * 96 + half * 48 : j * 96 + half * 48 + 48]
+    def up_grad(n, c):
+        chunk, side = n // 2, n % 2
+        put(4 + chunk, side, tn(low[...], slope[:, lanes(side * (ff // 2) + chunk * 384, 384)]))
+        return c
+    lax.fori_loop(0, 8, up_grad, 0)
+    reload("x", x_h, low)
+    pipe.move(3)
+    loads["wup"].wait()
+    def first_grad(n, c):
+        unit2[:, lanes(n * QUAD, QUAD)] += nt(slope[...], wup[pl.ds(pl.multiple_of(n * QUAD, QUAD), QUAD), :])
+        return c
+    lax.fori_loop(0, width // QUAD, first_grad, 0)
+    reload("cwup", cw_up, wup)
+    later[2].wait()
+    pipe.move(4)
+
+    n = 128
+    unit1_all = jnp.concatenate([buf[k // 16, k // 8 % 2, k // 4 % 2, k % 4, :, :width] for k in range(32)], 0)
+    unit2_all = jnp.concatenate([buf[k // 16, k // 8 % 2, k // 4 % 2, k % 4, :, width : 2 * width] for k in range(32)], 0)
+    base[0] = unit1_all
+    base[1] = unit2_all
+    cross_cot[...] = jnp.concatenate([buf[k // 16, k // 8 % 2, k // 4 % 2, k % 4, :, 2 * width : 3 * width] for k in range(32)], 0)
+    inv_all = jnp.concatenate([buf[k // 16, k // 8 % 2, k // 4 % 2, k % 4, :, 3 * width :] for k in range(32)], 0)[:, :1]
+    slot_c, place_c, doc_c, rank_c, first_c = row_docs((n, 1), 0, counts)
+    slot_r, place_r, doc_r, rank_r, first_r = row_docs((1, n), 1, counts)
+    places = lax.broadcasted_iota(jnp.int32, (32, n), 0)
+    by_slot = exact(pads[...].astype(F32), (places == place_r).astype(F32))
+    pad_r = jnp.zeros((1, n), F32)
+    for s in range(pads.shape[0]):
+        pad_r = jnp.where(slot_r == s, by_slot[s : s + 1], pad_r)
+    allowed = (slot_c == slot_r) & (doc_c == doc_r) & ((pad_r == 0) | (first_r == 1))
+    pick = (rank_c == lax.broadcasted_iota(jnp.int32, (n, 32), 1)).astype(F32)
+    xin = base[1] * gf + exact(pick, embed[...])
+    xl = xin.astype(BF16)
+    masks = head_mask(n)
+    wide = jnp.concatenate([allowed.astype(F32)] * 4, 0) > 0
+    loads["cwin"].wait()
+    cqkv = jnp.concatenate([nn(xl, win[:, k * width : (k + 1) * width]).astype(BF16) for k in range(3)], 1)
+    cprobs, catts = [], []
+    part = lambda a, k, quad: a[:, k * width + quad * QUAD : k * width + quad * QUAD + QUAD]
+    for quad in range(3):
+        scores = jnp.where(wide, nt(stacked(part(cqkv, 0, quad), masks), part(cqkv, 1, quad)) * HD ** -0.5, MASKED)
+        e = jnp.exp(scores - jnp.max(scores, -1, keepdims=True))
+        p = e / jnp.sum(e, -1, keepdims=True)
+        cprobs.append(p)
+        catts.append(picked(nn(p.astype(BF16), part(cqkv, 2, quad)), masks).astype(BF16))
+    catt = jnp.concatenate(catts, 1)
+    loads["cwproj"].wait()
+    u1, i1 = unit(xin + nn(catt, wproj[...]))
+    f = u1 * cga
+    fl = f.astype(BF16)
+    pipe.move(5)
+    hid, dpre, slp = slice(0, n), slice(n, 2 * n), slice(2 * n, 3 * n)
+    again["cwup"].wait()
+    def up(k, c):
+        s = lanes(k * tile, tile)
+        h, gl = gelu_pair(nn(fl, wup[:, s]))
+        hidden[hid, s] = h.astype(BF16)
+        hidden[slp, s] = gl.astype(BF16)
+        return c
+    lax.fori_loop(0, ff // tile, up, 0)
+    again["cwdown"].wait()
+    u2, i2 = unit(f + nn(hidden[hid, :], wdown[...]))
+    me = ((core * 2 + x_at) * 2 + y) * 4 + z
+    own = (lax.broadcasted_iota(jnp.int32, (8, n), 1) == 4 * me + lax.broadcasted_iota(jnp.int32, (8, n), 0)).astype(F32)
+    result = exact(own, u2 * cgf)
+    for s in range(segs):
+        r = slice(s * length, s * length + 16)
+        outb[r, :] = jnp.where(top[:16], result[s : s + 1], outb[r, :].astype(F32)).astype(BF16)
+    saves = [pltpu.make_async_copy(outb, out_o, out_sem.at[0])]
+    saves[0].start()
+    d2, cgain_f = norm_back(u2, i2, cross_cot[...], cgf)
+    dy2 = d2.astype(BF16)
+    pipe.move(6)
+    def pre(k, c):
+        s = lanes(k * tile, tile)
+        hidden[dpre, s] = (nt(dy2, wdown[pl.ds(pl.multiple_of(k * tile, tile), tile), :]) * hidden[slp, s].astype(F32)).astype(BF16)
+        return c
+    lax.fori_loop(0, ff // tile, pre, 0)
+    reload("wdown", w_down, wdown)
+    d1, cgain_a = norm_back(u1, i1, d2 + nt(hidden[dpre, :], wup[...]), cga)
+    reload("wup", w_up, wup)
+    dy1 = d1.astype(BF16)
+    datt = nt(dy1, wproj[...]).astype(BF16)
+    reload("wproj", w_proj, wproj)
+    dq, dk, dv = [], [], []
+    for quad in range(3):
+        da = stacked(part(datt, 0, quad), masks)
+        q, k = stacked(part(cqkv, 0, quad), masks), part(cqkv, 1, quad)
+        p = cprobs[quad]
+        dp = nt(da, part(cqkv, 2, quad))
+        ds = (p * (dp - jnp.sum(p * dp, -1, keepdims=True))).astype(BF16)
+        dq.append((picked(nn(ds, k), masks) * HD ** -0.5).astype(BF16))
+        dk.append((tn(ds, q) * HD ** -0.5).astype(BF16))
+        dv.append(tn(p.astype(BF16), da).astype(BF16))
+    dqkv = jnp.concatenate(dq + dk + dv, 1)
+    crossed = d1 + nt(dqkv, win[...])
+    reload("win", w_in, win)
+    pipe.move(7)
+
+    unit2_0 = base[1]
+    d20, spare = norm_back(unit2_0, inv_all, crossed, gf)
+    mine_up, mine_d2 = exact(own, crossed), exact(own, d20)
+    gains[1:2, :] += jnp.sum((mine_up * exact(own, unit2_0))[:segs], 0, keepdims=True)
+    dy0 = d20.astype(BF16)
+    mine_dy = mine_d2.astype(BF16)
+    f0 = (base[0] * ga).astype(BF16)
+    i, j = 2 * y + x_at, 2 * z + core
+    def turn(a, by):
+        a = a.astype(F32)
+        return pltpu.roll(a, lax.rem(a.shape[1] - by, a.shape[1]), 1).astype(BF16)
+    sixth = width // 8
+    left = lambda a: turn(a, sixth * j)[:, :128]
+    again["wdown"].wait()
+    again["wup"].wait()
+    quarter, eighth = ff // 4, ff // 8
+    hid0, spare = gelu_pair(nn(f0, wup[:, lanes(eighth * j, eighth)]))
+    d_down0[...] = tn(hid0.astype(BF16), turn(dy0, width // 4 * i)[:, :256])[:, : width // 4]
+    spare, slope_0 = gelu_pair(nn(f0, wup[:, lanes(quarter * i, quarter)]))
+    du0 = (nt(dy0, wdown[pl.ds(pl.multiple_of(quarter * i, quarter), quarter), :]) * slope_0).astype(BF16)
+    d_up0[...] = tn(left(f0), du0)[:sixth]
+    def mine_pre(k, d):
+        s = lanes(k * tile, tile)
+        du = (nt(mine_dy, wdown[pl.ds(pl.multiple_of(k * tile, tile), tile), :]) * slope0[:, s]).astype(BF16)
+        return d + nt(du, wup[:, s])
+    mine_first = lax.fori_loop(0, ff // tile, mine_pre, mine_d2)
+    for s in range(segs):
+        unit2[s * length : s * length + 1, :] = mine_first[s : s + 1]
+
+    def first(k, c):
+        r = pl.ds(pl.multiple_of(k * length, length), length)
+        d, gain = norm_back(unit1[r, :], inv[0, r, :1], unit2[r, :], ga)
+        gains[0:1, :] += gain
+        unit1[r, :] = d
+        dy[r, :] = d.astype(BF16)
+        return c
+    lax.fori_loop(0, segs, first, 0)
+    red.gain[0] = gains[...]
+    loads["att"].wait()
+    def proj_grad(side, c):
+        put(slot_of(8), side, tn(att[...], dy[:, lanes(side * 384, 384)]))
+        return c
+    lax.fori_loop(0, 2, proj_grad, 0)
+    pipe.move(8)
+    red.gain_start(0)
+    again["wproj"].wait()
+    att[...] = nt(dy[...], wproj[...]).astype(BF16)
+    loads["qkv"].wait()
+    loads["probs"].wait()
+    def attend(k, c):
+        seg, quad = k // 3, k % 3
+        r = pl.ds(pl.multiple_of(seg * length, length), length)
+        qs, ks, vs = (lanes(m * width + quad * QUAD, QUAD) for m in range(3))
+        da = stacked(att[r, lanes(quad * QUAD, QUAD)], masks)
+        q, keys = stacked(qkv[r, qs], masks), qkv[r, ks]
+        plow = probs[k]
+        p = plow.astype(F32)
+        dp = nt(da, qkv[r, vs])
+        ds = (p * (dp - jnp.sum(p * dp, -1, keepdims=True))).astype(BF16)
+        qkv[r, qs] = (picked(nn(ds, keys), masks) * HD ** -0.5).astype(BF16)
+        qkv[r, ks] = (tn(ds, q) * HD ** -0.5).astype(BF16)
+        qkv[r, vs] = tn(plow, da).astype(BF16)
+        return c
+    lax.fori_loop(0, 6, attend, 0)
+    red.gain_done(0); red.gain_start(1)
+    pipe.move()
+    lax.fori_loop(6, 3 * segs, attend, 0)
+    red.gain_done(1); red.gain_start(2)
+    again["x"].wait()
+    for chunk in range(3):
+        def in_grad(side, c):
+            put(slot_of(9 + chunk), side, tn(low[...], qkv[:, lanes(side * (3 * width // 2) + chunk * 384, 384)]))
+            return c
+        lax.fori_loop(0, 2, in_grad, 0)
+        pipe.move(9 + chunk)
+    red.gain_done(2); red.gain_start(3)
+    again["win"].wait()
+    def token(k, c):
+        s = lanes(k * QUAD, QUAD)
+        cot[:, s] = (unit1[:, s] + nt(qkv[...], win[pl.ds(pl.multiple_of(k * QUAD, QUAD), QUAD), :])).astype(BF16)
+        return c
+    lax.fori_loop(0, width // QUAD, token, 0)
+    saves.append(pltpu.make_async_copy(cot, token_o, out_sem.at[1]))
+    saves[1].start()
+    pipe.move()
+    c_in[...] = tn(left(xl), turn(dqkv, 3 * width // 4 * i)[:, :640])[:sixth, : 3 * width // 4]
+    c_proj[...] = tn(left(catt), turn(dy1, width // 4 * i)[:, :256])[:sixth, : width // 4]
+    c_up[...] = tn(left(fl), hidden[dpre, lanes(quarter * i, quarter)])[:sixth]
+    c_down[...] = tn(hidden[hid, lanes(eighth * j, eighth)], turn(dy2, width // 4 * i)[:, :256])[:, : width // 4]
+    pick8 = (rank_c - 8 * i == lax.broadcasted_iota(jnp.int32, (n, 8), 1)).astype(F32)
+    by_rank = exact(pick8, crossed, (((0,), (0,)), ((), ())))
+    embed_o[...] = pltpu.roll(by_rank, lax.rem(width - sixth * j, width), 1)[:, :sixth]
+    pipe.move()
+    red.gain_done(3)
+    every = jnp.concatenate([red.gain[0], cgain_a, cgain_f, jnp.zeros((4, width), F32)], 0)
+    small_o[...] = pltpu.roll(every, lax.rem(width - sixth * j, width), 1)[:, :128]
+    while pipe.flying:
+        pipe.move()
+    saves += [pltpu.make_async_copy(red.own, own_o, out_sem.at[2]), pltpu.make_async_copy(red.peer, peer_o, out_sem.at[3])]
+    for s in saves[2:]: s.start()
+    for s in saves: s.wait()
+
+def finish(x, cot, counts, pads, embed, saved, segs, weights, cross_weights):
+    w_in, w_proj, ga, w_up, w_down, gf = weights
+    cw_in, cw_proj, cga, cw_up, cw_down, cgf = cross_weights
+    rows, width = x.shape
+    ff = w_up.shape[1]
+    sixth = width // 8
+    outs = [((rows, width), BF16)] * 2 + [((NC, 48, 384), BF16)] * 2 + [((sixth, ff // 4), F32), ((ff // 8, width // 4), F32),
+            ((sixth, 3 * width // 4), F32), ((sixth, width // 4), F32), ((sixth, ff // 4), F32), ((ff // 8, width // 4), F32),
+            ((8, 128), F32), ((8, sixth), F32)]
+    dma = pltpu.SemaphoreType.DMA
+    v = lambda *s: pltpu.VMEM(s, BF16)
+    return pl.pallas_call(
+        partial(finish_kernel, segs), out_shape=[sds(*o) for o in outs],
+        in_specs=[ANY, ANY, pl.BlockSpec(memory_space=pltpu.SMEM), VM, VM, ANY, ANY, ANY, ANY, VM, VM, ANY, ANY, ANY, ANY, VM, VM] + [ANY] * 8,
+        out_specs=[ANY] * 4 + [VM] * 8,
+        scratch_shapes=[v(rows, width)] + [pltpu.VMEM(w.shape, BF16) for w in (w_in, w_proj, w_up, w_down)]
+        + [pltpu.VMEM(s.shape, s.dtype) for s in saved]
+        + [v(rows, width)] * 3 + [v(GS, 2, 2, 2, 2, 2, 48, 384), pltpu.VMEM((segs, PAY), F32), pltpu.VMEM((2, 2, 2, 4, segs, PAY), F32),
+           pltpu.VMEM((8, ff), F32), pltpu.VMEM((2, 128, width), F32), pltpu.VMEM((128, width), F32), pltpu.VMEM((2, width), F32),
+           dma((13,)), dma((7,)), dma((4,)), dma((1,)), dma((6,)), dma((6,))]
+        + Reducer.scratch(width),
+        compiler_params=pltpu.CompilerParams(collective_id=0, has_side_effects=True, vmem_limit_bytes=67043328), name="finish",
+    )(x, cot, counts, pads, embed, w_in, w_proj, w_up, w_down, ga, gf, cw_in, cw_proj, cw_up, cw_down, cga, cgf, *saved)
+
+def deliver_kernel(own, peer, d_up0, d_down0, small, token_i, out_i, ci_in, ci_proj, ci_up, ci_down, ci_embed,
+                   d_in, d_proj, d_up, d_down, g0, g1, g2, g3, token_o, out_o, c_in, c_proj, c_up, c_down, embed_o, token, out, sem):
+    big = [(token_i, token, token_o), (out_i, out, out_o)]
+    loads = [pltpu.make_async_copy(a, b, sem.at[k]) for k, (a, b, c) in enumerate(big)]
+    stores = [pltpu.make_async_copy(b, c, sem.at[2 + k]) for k, (a, b, c) in enumerate(big)]
+    for load in loads: load.start()
+    at = lax.rem(lax.axis_index("dp"), 2)
+    for mine in (0, 1):
+        @pl.when(at == mine)
+        def _():
+            for half in (0, 1):
+                a = own if half == mine else peer
+                r = slice(48 * half, 48 * half + 48)
+                side = slice(192 * mine, 192 * mine + 192)
+                d_proj[r, :] = a[8, :, side].astype(F32)
+                for k in range(2):
+                    s = slice(384 * k, 384 * k + 384)
+                    d_up[r, s] = a[4 + 2 * mine + k].astype(F32) + d_up0[r, s]
+                parts = [a[9], a[10, :, side]] if mine == 0 else [a[10, :, side], a[11]]
+                d_in[r, :] = jnp.concatenate(parts, 1).astype(F32)
+                for k in range(4):
+                    s = slice(96 * k + 48 * half, 96 * k + 48 * half + 48)
+                    d_down[s, :] = a[k, :, side].astype(F32) + d_down0[s, :]
+    for load, store in zip(loads, stores):
+        load.wait(); store.start()
+    for k, o in enumerate((g0, g1, g2, g3)):
+        o[...] = small[k : k + 1, : o.shape[0]].reshape(o.shape)
+    for a, b in ((ci_in, c_in), (ci_proj, c_proj), (ci_up, c_up), (ci_down, c_down), (ci_embed, embed_o)):
+        b[...] = a[...]
+    for store in stores: store.wait()
+
+def deliver(token, out, own, peer, d_up0, d_down0, c_in, c_proj, c_up, c_down, small, embed):
+    width = token.shape[1]
+    sixth = width // 8
+    like = lambda a: sds(a.shape, a.dtype)
+    outs = [sds((sixth, 3 * width // 4), F32), sds((sixth, width // 4), F32), like(d_up0), like(d_down0)] + [sds((sixth,), F32)] * 4 + [
+        like(a) for a in (token, out, c_in, c_proj, c_up, c_down, embed)]
+    return pl.pallas_call(
+        deliver_kernel, out_shape=outs, in_specs=[VM] * 5 + [ANY, ANY] + [VM] * 5, out_specs=[VM] * 8 + [ANY, ANY] + [VM] * 5,
+        scratch_shapes=[pltpu.VMEM(token.shape, BF16)] * 2 + [pltpu.SemaphoreType.DMA((4,))],
+        compiler_params=pltpu.CompilerParams(vmem_limit_bytes=20 << 20), name="deliver",
+    )(own, peer, d_up0, d_down0, small, token, out, c_in, c_proj, c_up, c_down, embed)
+
+
+def this_mesh(
+    tokens, doc_counts, pad_mask, attn_in, attn_proj, norm_attn, ffn_up, ffn_down, norm_ffn,
+    segment_embed, cross_in, cross_proj, cross_norm_attn, cross_up, cross_down, cross_norm_ffn,
+    cotangent,
+):
+    segs, length, width = tokens.shape
+    x, cot = tokens.reshape(segs * length, width), cotangent.reshape(segs * length, width)
+    weights = (attn_in, attn_proj, norm_attn, ffn_up, ffn_down, norm_ffn)
+    cross_weights = (cross_in, cross_proj, cross_norm_attn, cross_up, cross_down, cross_norm_ffn)
+    saved = forward(x, segs, weights)
+    done = finish(x, cot, doc_counts, pad_mask, segment_embed, saved, segs, weights, cross_weights)
+    d_in, d_proj, d_up, d_down, n_attn, n_ffn, c_attn, c_ffn, token, out, c_in, c_proj, c_up, c_down, embed = deliver(*done)
+    return (
+        out.reshape(tokens.shape), token.reshape(tokens.shape), d_in, d_proj, n_attn, d_up, d_down, n_ffn,
+        embed, c_in, c_proj, c_attn, c_up, c_down, c_ffn,
+    )
+
+
 def solution(mesh):
+    fits = (mesh.shape["dp"], mesh.shape["seg"]) == (4, 8)
     placed = (
         P(("dp", "seg"), None, None),
         P(),
@@ -296,7 +983,7 @@
         P(("dp", "seg"), None, None),
     )
     return jax.shard_map(
-        on_device,
+        this_mesh if fits else any_mesh,
         mesh=mesh,
         in_specs=placed,
         out_specs=(

time: 574 us -> 168 us (0.29); the launches traced: 567 us -> 167 us
  Pallas kernels: 0 us -> 154 us
  blocking collectives: 135 us -> 0 us
  matrix products: 132 us -> 0 us
  waiting for transfers between devices: 118 us -> 0 us
  local copies, waits for them, and re-layouts: 127 us -> 13.1 us
  other arithmetic: 39.2 us -> 0 us
  between operations: 15 us -> 0.69 us
    pallas_call x0 -> x3, Pallas kernels: none -> 154 us  [the longest x1 122 us: finish(): pl.pallas_call(partial(finish_kernel, segs), out_shape=[sds(*o) for o in...]
    dot_general x38 -> x0, matrix products: 132 us -> none  [the longest x8 40.2 us: matmul(): return jnp.dot(former, latter, preferred_element_type=jnp.float32)]
    all_gather x2 -> x0, blocking collectives: 95.1 us -> none  [the longest x1 50.2 us: on_device(): lax.all_gather(cotangent[:, 0, :], ('dp', 'seg'), axis=0, tiled=True)[order]]
    reduce_scatter x3 -> x0, waiting for transfers between devices: 83.3 us -> none  [reduce_weights(): lax.psum_scatter(g.astype(jnp.bfloat16), 'seg', scatter_dimension=0, tile...]
    reshape x19 -> x0, local copies, waits for them, and re-layouts: 41.6 us -> none  [the longest x8 18.4 us: to_heads(): return columns.reshape(batch_size, -1, H, HD)]
    psum x1 -> x0, blocking collectives: 40.4 us -> none  [on_device(): lax.psum(jnp.concatenate([grad_norm_attn, grad_norm_ffn]), ('dp', 'seg'))]
    unnamed x7 -> x0, waiting for transfers between devices: 35.2 us -> none
    slice x15 -> x0, local copies, waits for them, and re-layouts: 22.2 us -> none  [the longest x6 9.18 us: reduce_weights(): outs.append(joined[at:at + rows * columns].reshape(rows, columns))]
  transfers between devices with their start and end apart: 5 -> 0, of which waited for: 3 -> 0; matrix products, arithmetic and copies ran while one was open for 16% -> 0% of each run, Pallas kernels for 0% -> 0%
where the time goes in v3:
time: 168 us; the launch traced here: 167 us
  Pallas kernels  154 us (92%)
  local copies, waits for them, and re-layouts  13.1 us (8%)
    pallas_call x1, Pallas kernels, finish(): pl.pallas_call(partial(finish_kernel, segs), out_shape=[sds(*o) for o in...  122 us
    pallas_call x1, Pallas kernels, forward(): pl.pallas_call(partial(forward_kernel, segs), out_shape=[sds(*s) for s in...  28.8 us
    unnamed x26, local copies, waits for them, and re-layouts  13.1 us

profile of v3, /device:TPU:0, one launch (start us, length us, event | category | flops | bytes accessed | tf_op | source)
XLA Modules:
  0.0 167.5 jit_solution(18143153112988586126)
XLA Ops:
  0.6 28.8 %segment_forward.1 = (bf16[512,2304]{1,0:T(8,128)(2,1)}, bf16[12,512,128]{2,1,0:T(8,128)(2,1)}, bf16[512,768]{1,0:T(8,128)(2,1)}, f32[512,768]{1,0:T(8,128)}, f3...) custom-call(bf16[512,768]{1,0:T(8,128)(2,1)} %bitcast.4, ...), custom_call_target="tpu_custom_call" | custom-call | tf_op jit(solution)/shard_map/segment_forward/pallas_call | solution.py:415
  29.5 122.4 %finish.1 = (bf16[512,768]{1,0:T(8,128)(2,1)}, bf16[512,768]{1,0:T(8,128)(2,1)}, bf16[12,48,384]{2,1,0:T(8,128)(2,1)}, bf16[12,48,384]{2,1,0:T(8,128)(2,1)}, f32...) custom-call(bf16[512,768]{1,0:T(8,128)(2,1)} %bitcast.5, ...), custom_call_target="tpu_custom_call" | custom-call | tf_op jit(solution)/shard_map/finish/pallas_call | solution.py:889
  151.9 0.0 copy-start
  151.9 1.1 copy-done
  153.0 0.0 copy-start.1
  153.0 1.1 copy-done.1
  154.2 0.0 copy-start.2
  154.2 1.0 copy-done.2
  155.2 0.0 copy-start.3
  155.2 1.0 copy-done.3
  156.2 0.0 copy-start.4
  156.2 1.0 copy-done.4
  157.2 0.0 copy-start.5
  157.2 1.0 copy-done.5
  158.2 0.0 copy-start.6
  158.2 1.0 copy-done.6
  159.2 0.0 copy-start.7
  159.2 1.0 copy-done.7
  160.1 0.0 copy-start.8
  160.1 0.9 copy-done.8
  161.1 0.0 copy-start.9
  161.1 0.9 copy-done.9
  162.0 0.0 copy-start.10
  162.0 0.7 copy-done.10
  162.6 0.0 copy-start.11
  162.6 0.7 copy-done.11
  163.3 2.4 %deliver.1 = (f32[96,576]{1,0:T(8,128)}, f32[96,192]{1,0:T(8,128)}, f32[96,768]{1,0:T(8,128)}, f32[384,192]{1,0:T(8,128)S(1)}, f32[96]{0:T(128)}, /*index=5*/f32...) custom-call(bf16[12,48,384]{2,1,0:T(8,128)(2,1)S(1)} %copy-done.2, ...), custom_call_target="tpu_custom_call" | custom-call | tf_op jit(solution)/shard_map/deliver/pallas_call | solution.py:939
  165.7 0.9 copy.32
  166.6 0.9 copy.33
Async XLA Ops:
  151.9 1.1 copy-start
  153.0 1.1 copy-start.1
  154.2 1.0 copy-start.2
  155.2 1.0 copy-start.3
  156.2 1.0 copy-start.4
  157.2 1.0 copy-start.5
  158.2 1.0 copy-start.6
  159.2 1.0 copy-start.7
  160.1 0.9 copy-start.8
  161.1 0.9 copy-start.9
  162.0 0.7 copy-start.10
  162.6 0.7 copy-start.11
